TPU v7x, 512 devices: a whole 4x4x16 slice. The times are simulated.
512 devices in a mesh: expert: 64 (over y, z), dp: 8 (over x, core).
Axes of the slice: x: 4, y: 4, z: 16, core: 2. Of those that a mesh axis runs over, the one named last changes fastest.
Arguments:
- tokens: bfloat16 [2048, 2048], P('expert', 'dp'), may hold values from -6 to 6
- cotangent: bfloat16 [2048, 2048], P('expert', 'dp'), may hold values from -6 to 6
- routes: int32 [2048, 8], P('expert'), may hold values from 0 to 63, all different within a row; in each aligned block of 32 rows (0 to 31, 32 to 63, ...) at most 5 rows name the same one
- route_weights: bfloat16 [2048, 8], P('expert'), may hold values from 0.019897461 to 0.5
- gate_weight: bfloat16 [64, 1536, 2048], P('expert', 'dp'), may hold values from -6 to 6
- up_weight: bfloat16 [64, 1536, 2048], P('expert', 'dp'), may hold values from -6 to 6
- down_weight: bfloat16 [64, 1536, 2048], P('expert', 'dp'), may hold values from -6 to 6
- cluster_order: int32 [64], replicated, may hold values from 0 to 63, each once
Outputs:
- merged_gate: bfloat16 [64, 1536, 2048], P('expert', 'dp')
- merged_up: bfloat16 [64, 1536, 2048], P('expert', 'dp')
- merged_down: bfloat16 [64, 1536, 2048], P('expert', 'dp')
Inputs may be any that keep to these rules, and one draw needn't show every extreme that they name: `routes`: each row names 8 different experts. Among the 32 rows of one index of expert, no expert is named more than 5 times, a bound that some block reaches. `cluster_order`: each value appears once, so every cluster has exactly 4 experts.
All inputs are finite; a program needn't handle non-finite values.
Results may differ from a plain program's by a relative error of at most 0.0085.
Values may be sent and summed in bfloat16 or wider, within the bound.
No kernel may reach another device: no remote copies, remote signals or barrier semaphores. Data moves between devices by JAX's collectives and lax.ppermute only.
A program may use at most 64 MiB of HBM per device.

v0:
```python
import jax
import jax.numpy as jnp
from jax import lax
from jax.sharding import PartitionSpec as P

D = 2048
FF = 1536
MEMBERS = 4


fisher_floor = 1e-06


def silu_parts(values_in):
    sigmoid_val = jax.nn.sigmoid(values_in)
    return (values_in * sigmoid_val, sigmoid_val * (1.0 + values_in * (1.0 - sigmoid_val)))


def contract_rows(left_side, right_side):
    return lax.dot_general(
        left_side, right_side, (((0,), (0,)), ((), ())), preferred_element_type=jnp.float32
    )


def project(rows_in, weight_in):
    return lax.dot_general(
        rows_in, weight_in, (((1,), (1,)), ((), ())), preferred_element_type=jnp.float32
    )


def body(
    tokens, cotangent, routes, route_weights, gate_weight, up_weight, down_weight, cluster_order
):
    experts_all = lax.axis_size("expert")
    tok_count = routes.shape[0]
    top_count = routes.shape[1]
    capacity = max(2, (5 * tok_count * top_count + 4 * experts_all - 1) // (4 * experts_all))
    rows_total = experts_all * capacity
    flat_dest = routes.reshape(-1)
    one_hot = (flat_dest[:, None] == jnp.arange(experts_all, dtype=jnp.int32)[None, :]).astype(
        jnp.int32
    )
    earlier = jnp.cumsum(one_hot, axis=0) - one_hot
    slot_index = jnp.sum(earlier * one_hot, axis=1)
    target_row = (flat_dest * capacity + slot_index).reshape(tok_count, top_count)
    row_ids = jnp.arange(rows_total, dtype=jnp.int32)
    matches = target_row[None, :, :] == row_ids[:, None, None]
    placement_matrix = jnp.any(matches, axis=2).astype(jnp.bfloat16)
    slot_weight = (
        jnp.sum(jnp.where(matches, route_weights.astype(jnp.float32)[None, :, :], 0.0), axis=(1, 2))
        .astype(jnp.bfloat16)
        .reshape(experts_all, capacity)
    )

    def scatter_rows(source_rows):
        placed = jnp.dot(placement_matrix, source_rows, preferred_element_type=jnp.float32)
        return placed.astype(jnp.bfloat16).reshape(experts_all, capacity, source_rows.shape[1])

    recv_tok, recv_cot, recv_weight = (
        lax.all_to_all(scatter_rows(tokens), "expert", split_axis=0, concat_axis=0, tiled=True),
        lax.all_to_all(scatter_rows(cotangent), "expert", split_axis=0, concat_axis=0, tiled=True),
        lax.all_to_all(slot_weight, "expert", split_axis=0, concat_axis=0, tiled=True),
    )
    full_tok, full_cot = (
        lax.all_gather(recv_tok.reshape(rows_total, tokens.shape[1]), "dp", axis=1, tiled=True),
        lax.all_gather(recv_cot.reshape(rows_total, tokens.shape[1]), "dp", axis=1, tiled=True),
    )
    row_weight = recv_weight.reshape(rows_total)
    gate_local = gate_weight[0]
    up_local = up_weight[0]
    down_local = down_weight[0]
    hidden_local = gate_local.shape[0]
    gate_pre = project(full_tok, gate_local) * D ** (-0.5)
    up_pre = project(full_tok, up_local) * D ** (-0.5)
    silu_value, silu_slope = silu_parts(gate_pre)
    activation = silu_value * up_pre
    out_grad = (row_weight.astype(jnp.float32)[:, None] * full_cot.astype(jnp.float32)).astype(
        jnp.bfloat16
    )
    act_grad = project(out_grad, down_local) * FF ** (-0.5)
    up_grad = act_grad * silu_value
    gate_grad = act_grad * up_pre * silu_slope
    tok_float = full_tok.astype(jnp.float32)
    grad_float = out_grad.astype(jnp.float32)
    tok_sq = (tok_float * tok_float).astype(jnp.bfloat16)
    grad_sq = (grad_float * grad_float).astype(jnp.bfloat16)
    act_sq = (activation * activation).astype(jnp.bfloat16)
    gate_sq = (gate_grad * gate_grad).astype(jnp.bfloat16)
    up_sq = (up_grad * up_grad).astype(jnp.bfloat16)
    fisher_gate = contract_rows(gate_sq, tok_sq).astype(jnp.bfloat16)
    fisher_up = contract_rows(up_sq, tok_sq).astype(jnp.bfloat16)
    fisher_down = contract_rows(act_sq, grad_sq).astype(jnp.bfloat16)
    weights_stack = jnp.concatenate([gate_weight, up_weight, down_weight], axis=0)
    fisher_stack = jnp.stack([fisher_gate, fisher_up, fisher_down], axis=0)
    element_count = 3 * hidden_local * D
    weights_flat = weights_stack.reshape(1, experts_all, element_count // experts_all)
    fisher_flat = fisher_stack.reshape(1, experts_all, element_count // experts_all)
    cluster_ids = cluster_order // MEMBERS
    same_cluster = (cluster_ids[:, None] == cluster_ids[None, :]).astype(jnp.float32)
    weight_part = lax.all_to_all(weights_flat, "expert", split_axis=1, concat_axis=0, tiled=True)
    fisher_part = lax.all_to_all(fisher_flat, "expert", split_axis=1, concat_axis=0, tiled=True)
    fisher_value = fisher_part.astype(jnp.float32)
    numerator = jnp.einsum(
        "st,tin->sin",
        same_cluster,
        fisher_value * weight_part.astype(jnp.float32),
        precision=lax.Precision.HIGHEST,
    )
    denominator = (
        jnp.einsum("st,tin->sin", same_cluster, fisher_value, precision=lax.Precision.HIGHEST)
        + fisher_floor
    )
    merged = (numerator / denominator).astype(jnp.bfloat16)
    merged_flat = lax.all_to_all(merged, "expert", split_axis=0, concat_axis=1, tiled=True)
    merged_stack = merged_flat.reshape(3, hidden_local, D)
    return (merged_stack[0:1], merged_stack[1:2], merged_stack[2:3])


def solution(mesh):
    return jax.shard_map(
        body,
        mesh=mesh,
        in_specs=(
            P("expert", "dp"),
            P("expert", "dp"),
            P("expert", None),
            P("expert", None),
            P("expert", "dp", None),
            P("expert", "dp", None),
            P("expert", "dp", None),
            P(),
        ),
        out_specs=(P("expert", "dp", None), P("expert", "dp", None), P("expert", "dp", None)),
        check_vma=False,
    )
```

profile of v0, /device:TPU:6, one launch (start us, length us, event | category | flops | bytes accessed | tf_op | source)
XLA Modules:
  0.0 534.1 jit_solution(8945066053835747545)
XLA Ops:
  7.2 0.0 copy-start
  7.2 0.8 copy.37
  7.9 0.1 eq.58
  8.0 0.1 eq.54
  8.1 0.8 copy.41
  8.9 0.6 reduce-window.6
  9.5 0.2 slice_reduce_fusion
  9.7 0.1 fusion.20
  9.9 0.1 reduce_sum.21
  10.0 0.2 select_reduce_fusion
  10.1 0.8 convert_element_type.127
  10.9 18.7 %all-to-all-start = ((bf16[64,1,5]{2,1,0:T(2,128)(2,1)}), bf16[64,1,5]{2,1,0:T(2,128)(2,1)S(1)}, u32[]{:S(2)}, u32[]{:S(2)}) async-start(bf16[64,1,5]{2,1,0:T(2,128)(2,1)} %convert_element_type.127), calls=%async_computation | async-start | bytes 65536 | tf_op jit(solution)/shard_map/all_to_all | solution.py:62
  29.6 0.2 fusion.15
  29.8 0.2 convolution_convert_fusion.3
  30.1 0.8 reshape.110
  30.9 13.1 %all-to-all-done = bf16[64,1,5]{2,1,0:T(2,128)(2,1)S(1)} async-done(((bf16[64,1,5]{2,1,0:T(2,128)(2,1)}), bf16[64,1,5]{2,1,0:T(2,128)(2,1)S(1)}, u32[]{:S(2)}, u32[]{:S(2)}) %all-to-all-start) | async-done | bytes 672 | tf_op jit(solution)/shard_map/all_to_all | solution.py:62
  44.0 4.6 all-to-all-start.2
  48.6 1.0 convolution_convert_fusion.4
  49.6 0.8 reshape.108
  50.4 18.1 %all-to-all-done.2 = bf16[64,5,256]{2,1,0:T(8,128)(2,1)S(1)} async-done(((bf16[64,5,256]{2,1,0:T(8,128)(2,1)}), bf16[64,5,256]{2,1,0:T(8,128)(2,1)S(1)}, u32[]{:S(2)}, u32[]{:S(2)}) %all-to-all-start.2) | async-done | bytes 163872 | tf_op jit(solution)/shard_map/all_to_all | solution.py:60
  68.5 6.4 %all-to-all-start.1 = ((bf16[64,5,256]{2,1,0:T(8,128)(2,1)}), bf16[64,5,256]{2,1,0:T(8,128)(2,1)S(1)}, u32[]{:S(2)}, u32[]{:S(2)}) async-start(bf16[64,5,256]{2,1,0:T(8,128)(2,1)} %reshape.108), calls=%async_computation.1 | async-start | bytes 524288 | tf_op jit(solution)/shard_map/all_to_all | solution.py:61
  74.9 1.9 pad_maximum_fusion.1
  76.8 5.6 %reshape.118 = bf16[1,64,18432]{2,0,1:T(2,128)(2,1)} reshape(bf16[3,192,2048]{2,1,0:T(8,128)(2,1)S(1)} %pad_maximum_fusion.1) | data formatting | bytes 4718592 | tf_op jit(solution)/shard_map/reshape | solution.py:96
  82.4 0.5 broadcast.61
  82.9 14.8 %reduce.8 = bf16[64,18432]{1,0:T(8,128)(2,1)S(1)} reduce(bf16[64,1,18432]{2,1,0:T(2,128)(2,1)} %bitcast.59, bf16[]{:T(256)} %broadcast.61), dimensions={1}, to_apply=%bitcast.50.reduce_sub_computation | reduce | bytes 4718594
  97.7 3.0 reshape.130
  100.7 15.1 %all-to-all-start.4 = ((bf16[64,2,9216]{2,1,0:T(2,128)(2,1)}), bf16[64,2,9216]{2,1,0:T(2,128)(2,1)S(1)}, u32[]{:S(2)}, u32[]{:S(2)}) async-start(bf16[64,2,9216]{2,1,0:T(2,128)(2,1)} %reshape.130), calls=%async_computation.4 | async-start | bytes 4718592 | tf_op jit(solution)/shard_map/all_to_all | solution.py:100
  115.8 0.0 all-gather.5.cloned.1.call-start
  115.9 0.7 reshape.111
  116.6 0.0 all-gather.5.cloned.1.call-update
  116.6 0.2 all-gather.3.cloned.1.call-start
  116.9 0.7 reshape.109
  117.6 0.0 all-gather.3.cloned.1.call-update
  117.6 0.1 convert_reduce_fusion
  117.7 0.1 reshape.115
  117.9 33.3 %all-gather.5.cloned.1.call-done = bf16[320,2048]{1,0:T(8,128)(2,1)} async-done(((bf16[320,256]{1,0:T(8,128)(2,1)}), bf16[320,2048]{1,0:T(8,128)(2,1)}) %all-gather.5.cloned.1.call-update) | async-done | bytes 1310736 | tf_op jit(solution)/shard_map/all_gather | solution.py:65
  151.2 2.2 convolution_multiply_fusion
  153.4 33.2 %all-gather.3.cloned.1.call-done = bf16[320,2048]{1,0:T(8,128)(2,1)} async-done(((bf16[320,256]{1,0:T(8,128)(2,1)}), bf16[320,2048]{1,0:T(8,128)(2,1)}) %all-gather.3.cloned.1.call-update) | async-done | bytes 1310736 | tf_op jit(solution)/shard_map/all_gather | solution.py:66
  186.6 2.2 convolution_multiply_fusion.2
  188.8 0.0 copy-start.4
  188.8 0.6 fusion.4
  189.5 0.5 copy-done.4
  190.0 0.7 convolution_multiply_fusion.1
  190.6 0.7 fusion.3
  191.3 0.6 copy-done.6
  192.0 0.7 fusion.5
  192.7 1.7 pad_maximum_fusion
  194.4 7.8 %reshape.117 = bf16[1,64,18432]{2,0,1:T(2,128)(2,1)} reshape(bf16[3,192,2048]{2,1,0:T(8,128)(2,1)} %pad_maximum_fusion) | data formatting | bytes 4718592 | tf_op jit(solution)/shard_map/reshape | solution.py:97
  202.2 16.2 %reduce.7 = bf16[64,18432]{1,0:T(8,128)(2,1)} reduce(bf16[64,1,18432]{2,1,0:T(2,128)(2,1)} %bitcast.60, bf16[]{:T(256)} %broadcast.61), dimensions={1}, to_apply=%bitcast.48.reduce_sub_computation | reduce | bytes 4718594
  218.4 4.8 reshape.128
  223.1 16.2 %all-to-all-start.3 = ((bf16[64,2,9216]{2,1,0:T(2,128)(2,1)}), bf16[64,2,9216]{2,1,0:T(2,128)(2,1)}, u32[]{:S(2)}, u32[]{:S(2)}) async-start(bf16[64,2,9216]{2,1,0:T(2,128)(2,1)} %reshape.128), calls=%async_computation.3 | async-start | bytes 4718592 | tf_op jit(solution)/shard_map/all_to_all | solution.py:101
  239.4 6.8 %reshape.131 = bf16[64,1,18432]{2,1,0:T(2,128)(2,1)} reshape(bf16[64,2,9216]{2,1,0:T(2,128)(2,1)S(1)} %all-to-all-done.4) | data formatting | bytes 4718592
  246.1 102.5 %all-to-all-done.3 = bf16[64,2,9216]{2,1,0:T(2,128)(2,1)} async-done(((bf16[64,2,9216]{2,1,0:T(2,128)(2,1)}), bf16[64,2,9216]{2,1,0:T(2,128)(2,1)}, u32[]{:S(2)}, u32[]{:S(2)}) %all-to-all-start.3) | async-done | bytes 2359328 | tf_op jit(solution)/shard_map/all_to_all | solution.py:101
  348.6 10.5 %reshape.129 = bf16[64,1,18432]{2,1,0:T(2,128)(2,1)} reshape(bf16[64,2,9216]{2,1,0:T(2,128)(2,1)} %all-to-all-done.3) | data formatting | bytes 4718592
  359.1 4.5 convolution_add_fusion
  363.7 9.8 %fusion.1 = bf16[64,1,18432]{2,0,1:T(8,128)(2,1)} fusion(f32[64,18432]{1,0:T(8,128)S(1)} %convolution_add_fusion, bf16[1,64,18432]{2,0,1:T(2,128)(2,1)} %bitcast.63, bf16[1,64,18432]{2,0,1:T(2,128)(2,1)S(1)} %bitcast.62, s32[64]{0:T(128)S(1)} %and_select_fusion), kind=kOutput, calls=%fused_computation.3 | convolution fusion | flops 911872000 | bytes 11796736 | tf_op jit(solution)/shard_map/st,tin->sin/dot_general | solution.py:103
  373.5 4.2 reduce.9
  377.6 3.0 reshape.132
  380.6 118.2 %all_to_all.46 = bf16[64,2,9216]{2,1,0:T(2,128)(2,1)S(1)} all-to-all(bf16[64,2,9216]{2,1,0:T(2,128)(2,1)} %reshape.132), channel_id=1, replica_groups=mesh['expert'=64,'dp'=8] {'expert'}, dimensions={0} | all-to-all | bytes 4718592 | tf_op jit(solution)/shard_map/all_to_all | solution.py:114
  498.9 6.7 %reshape.133 = bf16[64,1,18432]{2,1,0:T(2,128)(2,1)} reshape(bf16[64,2,9216]{2,1,0:T(2,128)(2,1)S(1)} %all_to_all.46) | data formatting | bytes 4718592
  505.6 14.1 %reduce.2 = bf16[64,18432]{1,0:T(8,128)(2,1)S(1)} reduce(bf16[64,1,18432]{2,1,0:T(2,128)(2,1)} %reshape.133, bf16[]{:T(256)} %constant.44), dimensions={1}, to_apply=%all_to_all.39.reduce_sub_computation | reduce | bytes 4718594 | tf_op jit(solution)/shard_map/all_to_all | solution.py:114
  519.7 0.0 copy-start.1
  519.8 4.4 reshape.114
  524.2 3.1 fusion.33
  (18 shorter events, 0.1 us)
Async XLA Ops:
  7.2 22.7 %copy-start = (bf16[32,256]{1,0:T(8,128)(2,1)S(1)}, bf16[32,256]{1,0:T(8,128)(2,1)}, u32[]{:S(2)}) copy-start(bf16[32,256]{1,0:T(8,128)(2,1)} %param.8) | copy-start | bytes 49156
  10.9 33.1 %all-to-all-start = ((bf16[64,1,5]{2,1,0:T(2,128)(2,1)}), bf16[64,1,5]{2,1,0:T(2,128)(2,1)S(1)}, u32[]{:S(2)}, u32[]{:S(2)}) async-start(bf16[64,1,5]{2,1,0:T(2,128)(2,1)} %convert_element_type.127), calls=%async_computation | async-start | bytes 65536 | tf_op jit(solution)/shard_map/all_to_all | solution.py:62
  44.0 24.5 %all-to-all-start.2 = ((bf16[64,5,256]{2,1,0:T(8,128)(2,1)}), bf16[64,5,256]{2,1,0:T(8,128)(2,1)S(1)}, u32[]{:S(2)}, u32[]{:S(2)}) async-start(bf16[64,5,256]{2,1,0:T(8,128)(2,1)} %reshape.110), calls=%async_computation.2 | async-start | bytes 524288 | tf_op jit(solution)/shard_map/all_to_all | solution.py:60
  68.5 32.1 %all-to-all-start.1 = ((bf16[64,5,256]{2,1,0:T(8,128)(2,1)}), bf16[64,5,256]{2,1,0:T(8,128)(2,1)S(1)}, u32[]{:S(2)}, u32[]{:S(2)}) async-start(bf16[64,5,256]{2,1,0:T(8,128)(2,1)} %reshape.108), calls=%async_computation.1 | async-start | bytes 524288 | tf_op jit(solution)/shard_map/all_to_all | solution.py:61
  100.7 122.4 %all-to-all-start.4 = ((bf16[64,2,9216]{2,1,0:T(2,128)(2,1)}), bf16[64,2,9216]{2,1,0:T(2,128)(2,1)S(1)}, u32[]{:S(2)}, u32[]{:S(2)}) async-start(bf16[64,2,9216]{2,1,0:T(2,128)(2,1)} %reshape.130), calls=%async_computation.4 | async-start | bytes 4718592 | tf_op jit(solution)/shard_map/all_to_all | solution.py:100
  115.8 35.4 %all-gather.5.cloned.1.call-start = ((), (), s32[]{:S(2)}) async-start(), calls=%async_computation.7 | async-start | bytes 1474560 | tf_op jit(solution)/shard_map/all_gather | solution.py:65
  116.6 70.0 %all-gather.3.cloned.1.call-start = ((), (), s32[]{:S(2)}) async-start(), calls=%async_computation.6 | async-start | bytes 1474560 | tf_op jit(solution)/shard_map/all_gather | solution.py:66
  117.6 69.0 %copy-start.3 = (bf16[1,192,2048]{2,1,0:T(8,128)(2,1)S(1)}, bf16[1,192,2048]{2,1,0:T(8,128)(2,1)}, u32[]{:S(2)}) copy-start(bf16[1,192,2048]{2,1,0:T(8,128)(2,1)} %param.14) | copy-start | bytes 2359300
  186.6 2.2 copy-start.5
  188.8 1.1 copy-start.4
  190.6 1.3 copy-start.6
  223.1 16.2 %copy-start.7 = (s32[64]{0:T(128)S(1)}, s32[64]{0:T(128)}, u32[]{:S(2)}) copy-start(s32[64]{0:T(128)} %param.15) | copy-start | bytes 772
  223.1 125.5 %all-to-all-start.3 = ((bf16[64,2,9216]{2,1,0:T(2,128)(2,1)}), bf16[64,2,9216]{2,1,0:T(2,128)(2,1)}, u32[]{:S(2)}, u32[]{:S(2)}) async-start(bf16[64,2,9216]{2,1,0:T(2,128)(2,1)} %reshape.128), calls=%async_computation.3 | async-start | bytes 4718592 | tf_op jit(solution)/shard_map/all_to_all | solution.py:101
  359.1 4.6 copy-start.2
  519.7 7.5 %copy-start.1 = (bf16[32,256]{1,0:T(8,128)(2,1)S(1)}, bf16[32,256]{1,0:T(8,128)(2,1)}, u32[]{:S(2)}) copy-start(bf16[32,256]{1,0:T(8,128)(2,1)} %param.8) | copy-start | bytes 49156
Sparse Core Ops, SparseCore 0:
  119.3 31.8 all-gather.4
  153.9 32.6 all-gather.2
where the time goes:
time: 536 us; the launch traced here: 534 us
  waiting for transfers between devices  200 us (37%)
  blocking collectives  118 us (22%)
  local copies, waits for them, and re-layouts  63.1 us (12%)
  starting transfers between devices  61.4 us (11%)
  other arithmetic  54.1 us (10%)
  matrix products  22.7 us (4%)
  between operations  14.3 us (3%)
    all_to_all x1, blocking collectives, body(): lax.all_to_all(merged, 'expert', split_axis=0, concat_axis=1, tiled=True)  118 us
    all_to_all x1, waiting for transfers between devices, body(): lax.all_to_all(fisher_flat, 'expert', split_axis=1, concat_axis=0, tiled=...  102 us
    unnamed x24, local copies, waits for them, and re-layouts  37.2 us
    all_gather x1, waiting for transfers between devices, body(): lax.all_gather(recv_tok.reshape(rows_total, tokens.shape[1]), 'dp', axis=...  33.3 us
    all_gather x1, waiting for transfers between devices, body(): lax.all_gather(recv_cot.reshape(rows_total, tokens.shape[1]), 'dp', axis=...  33.2 us
    unnamed x2, other arithmetic  31 us
    all_to_all x1, starting transfers between devices, body(): lax.all_to_all(slot_weight, 'expert', split_axis=0, concat_axis=0, tiled=...  18.7 us
    all_to_all x1, waiting for transfers between devices, body(): lax.all_to_all(scatter_rows(tokens), 'expert', split_axis=0, concat_axis=...  18.1 us
  transfers between devices with their start and end apart: 7, of which 5 were waited for; matrix products, arithmetic and copies ran while one was open for 14% of the time, Pallas kernels for 0%

commit v1 on v0

v1 whole, which is shorter than its diff:
```python
import jax
import jax.numpy as jnp
from jax import lax
from jax.experimental import pallas as pl
from jax.experimental.pallas import tpu as pltpu
from jax.sharding import PartitionSpec as P

D = 2048
FF = 1536
MEMBERS = 4
EXPERTS = 64
CLUSTERS = 16
ROWS = 3
KINDS = 3 * ROWS
LANES = 128
TILES = D // LANES
BLOCK = 32
WIDTH = 256
Y, Z = 4, 16
fisher_floor = 1e-06
VMEM_LIMIT = 60 * 1024 * 1024


def swap_matrix():
    row = lax.broadcasted_iota(jnp.int32, (256, 256), 0)
    col = lax.broadcasted_iota(jnp.int32, (256, 256), 1)
    hit = (row // 16 == col % 16) & (row % 16 == col // 16)
    return jnp.where(hit, 1.0, 0.0).astype(jnp.bfloat16)


def dot(left, right):
    return jnp.dot(left, right, preferred_element_type=jnp.float32)


def dot_t(left, right):
    return lax.dot_general(
        left, right, (((1,), (1,)), ((), ())), preferred_element_type=jnp.float32
    )


def pack_kernel(gate, up, down, out):
    swap = swap_matrix()
    for m, ref in enumerate((gate, up, down)):
        for j in range(ROWS):
            for kb in range(4):
                rows = slice(64 * j + 16 * kb, 64 * j + 16 * kb + 16)
                stacked = jnp.concatenate(
                    [ref[rows, l * LANES : (l + 1) * LANES] for l in range(TILES)], axis=0
                )
                turned = dot(swap, stacked).astype(jnp.bfloat16)
                q = m * ROWS + j
                out[16 * kb : 16 * kb + 16, 16 * q : 16 * q + 16, :] = turned.reshape(
                    16, 16, LANES
                )


def unpack_kernel(packed, gate, up, down):
    swap = swap_matrix()
    for m, ref in enumerate((gate, up, down)):
        for j in range(ROWS):
            for kb in range(4):
                q = m * ROWS + j
                stacked = packed[16 * kb : 16 * kb + 16, 16 * q : 16 * q + 16, :].reshape(
                    256, LANES
                )
                turned = dot(swap, stacked).astype(jnp.bfloat16)
                rows = slice(64 * j + 16 * kb, 64 * j + 16 * kb + 16)
                for l in range(TILES):
                    ref[rows, l * LANES : (l + 1) * LANES] = turned[16 * l : 16 * l + 16]


def merge_kernel(*refs):
    (packed, route_map, members, spread) = refs[:4]
    pieces = refs[4:14]
    out, tok, cot, weights, fisher_rows, merged, sems = refs[14:]
    place = lax.axis_index("dp")
    x, core = place // 2, place % 2
    copies = []
    for side in range(2):
        c = core if side == 0 else 1 - core
        for i, (shift, first) in enumerate(((0, 0), (3, 0), (1, 0), (2, 0), (2, 32))):
            piece = pieces[5 * side + i]
            lane = pl.multiple_of((((x + shift) % 4) * 2 + c) * WIDTH, WIDTH)
            blocks = piece.shape[0]
            for h, target in enumerate((tok, cot)):
                copy = pltpu.make_async_copy(
                    piece.at[:, h * BLOCK : (h + 1) * BLOCK, :],
                    target.at[first : first + blocks, :, pl.ds(lane, WIDTH)],
                    sems.at[2 * (5 * side + i) + h],
                )
                copy.start()
                copies.append(copy)
    swap = swap_matrix()
    for q in range(KINDS):
        for eb in range(4):
            stacked = packed[16 * eb : 16 * eb + 16, 16 * q : 16 * q + 16, :].reshape(256, LANES)
            turned = dot(swap, stacked).astype(jnp.bfloat16)
            rows = slice(64 * q + 16 * eb, 64 * q + 16 * eb + 16)
            for l in range(TILES):
                weights[rows, l * LANES : (l + 1) * LANES] = turned[16 * l : 16 * l + 16]
    for copy in copies:
        copy.wait()
    third = ROWS * EXPERTS

    def project(t, carry):
        at = pl.multiple_of(t * 8, 8)
        tok_rows = tok[pl.ds(at, 8)].reshape(256, D)
        cot_rows = cot[pl.ds(at, 8)].reshape(256, D)
        lane = pl.multiple_of(t * 256, 256)
        share = route_map[:, pl.ds(lane, 256)]
        share = jnp.concatenate([share] * ROWS, axis=0)
        pre = dot_t(weights[0 : 2 * third, :], tok_rows) * (D**-0.5)
        act_grad = dot_t(weights[2 * third :, :], cot_rows) * (FF**-0.5) * share
        gate_pre, up_pre = pre[:third], pre[third:]
        sigmoid = jax.nn.sigmoid(gate_pre)
        silu = gate_pre * sigmoid
        slope = sigmoid * (1.0 + gate_pre * (1.0 - sigmoid))
        gate_grad = act_grad * up_pre * slope
        up_grad = act_grad * silu
        act = silu * up_pre * share
        for m, value in enumerate((gate_grad, up_grad, act)):
            fisher_rows[m * third : (m + 1) * third, pl.ds(lane, 256)] = (value * value).astype(
                jnp.bfloat16
            )
        return carry

    lax.fori_loop(0, 8, project, 0)

    def merge(f, carry):
        lane = pl.multiple_of(f * WIDTH, WIDTH)
        tok_cols = tok[:, :, pl.ds(lane, WIDTH)].reshape(2048, WIDTH)
        cot_cols = cot[:, :, pl.ds(lane, WIDTH)].reshape(2048, WIDTH)
        fisher_in = dot(fisher_rows[0 : 2 * third, :], tok_cols * tok_cols)
        fisher_down = dot(fisher_rows[2 * third :, :], cot_cols * cot_cols)
        fisher = jnp.concatenate(
            [fisher_in.astype(jnp.bfloat16), fisher_down.astype(jnp.bfloat16)], axis=0
        )
        product = fisher.astype(jnp.float32) * weights[:, pl.ds(lane, WIDTH)].astype(jnp.float32)
        high = product.astype(jnp.bfloat16)
        low = (product - high.astype(jnp.float32)).astype(jnp.bfloat16)
        table = members[...]
        numerator = dot(table, high) + dot(table, low)
        denominator = dot(table, fisher)
        merged[:, pl.ds(lane, WIDTH)] = (numerator / (denominator + fisher_floor)).astype(
            jnp.bfloat16
        )
        return carry

    lax.fori_loop(0, 8, merge, 0)
    for q in range(KINDS):
        stacked = jnp.concatenate(
            [merged[16 * q : 16 * q + 16, l * LANES : (l + 1) * LANES] for l in range(TILES)], axis=0
        )
        for eb in range(4):
            turned = dot(spread[256 * eb : 256 * eb + 256, :], stacked).astype(jnp.bfloat16)
            out[16 * eb : 16 * eb + 16, 16 * q : 16 * q + 16, :] = turned.reshape(16, 16, LANES)


def params():
    return pltpu.CompilerParams(vmem_limit_bytes=VMEM_LIMIT)


PACKED = jax.ShapeDtypeStruct((EXPERTS, KINDS * TILES, LANES), jnp.bfloat16)


def expert_pairs(move):
    return [(y * Z + z, move(y, z)[0] * Z + move(y, z)[1]) for y in range(Y) for z in range(Z)]


def dp_pairs(move):
    return [(2 * x + c, move(x, c)[0] * 2 + move(x, c)[1]) for x in range(4) for c in range(2)]


def gather_ring(value, axis, up, down):
    half = value.shape[0] // 2
    before = lax.ppermute(value, axis, up)
    after = lax.ppermute(value, axis, down)
    far_first = lax.ppermute(before[:half], axis, up)
    far_last = lax.ppermute(after[half:], axis, down)
    return value, before, after, far_first, far_last


def body(
    tokens, cotangent, routes, route_weights, gate_weight, up_weight, down_weight, cluster_order
):
    hidden = gate_weight.shape[1]
    whole = pl.BlockSpec(memory_space=pltpu.VMEM)
    packed = pl.pallas_call(
        pack_kernel, out_shape=PACKED, in_specs=[whole] * 3, out_specs=whole,
        compiler_params=params(), name="pack",
    )(gate_weight[0], up_weight[0], down_weight[0])
    received = lax.all_to_all(packed, "expert", split_axis=0, concat_axis=0, tiled=True)

    chosen = routes[:, :, None] == jnp.arange(EXPERTS, dtype=jnp.int32)[None, None, :]
    share = jnp.sum(jnp.where(chosen, route_weights.astype(jnp.float32)[:, :, None], 0.0), axis=1)
    share = share.astype(jnp.bfloat16)
    share = jnp.concatenate([share[8 * i : 8 * i + 8] for i in range(4)], axis=1)
    block = jnp.concatenate([tokens, cotangent, share], axis=0)[None]
    for bit in (8, 4, 2, 1):
        other = lax.ppermute(block, "expert", expert_pairs(lambda y, z: (y, z ^ bit)))
        block = jnp.concatenate([block, other], axis=0)
    ring = gather_ring(
        block, "expert",
        expert_pairs(lambda y, z: ((y + 1) % Y, z)), expert_pairs(lambda y, z: ((y - 1) % Y, z)),
    )
    block = jnp.concatenate(ring, axis=0)
    share = block[:, 2 * BLOCK :, :].reshape(EXPERTS, 8, 4, EXPERTS).transpose(3, 0, 2, 1)
    share = share.reshape(EXPERTS, EXPERTS * BLOCK).astype(jnp.float32)
    near = gather_ring(
        block[:, : 2 * BLOCK, :], "dp",
        dp_pairs(lambda x, c: ((x + 1) % 4, c)), dp_pairs(lambda x, c: ((x - 1) % 4, c)),
    )
    across = dp_pairs(lambda x, c: (x, 1 - c))
    pieces = near + tuple(lax.ppermute(piece, "dp", across) for piece in near)

    cluster = cluster_order // MEMBERS
    belongs = cluster[None, :] == jnp.arange(CLUSTERS, dtype=jnp.int32)[:, None]
    members = jnp.einsum("qp,ce->qcpe", jnp.eye(KINDS), belongs.astype(jnp.float32))
    members = members.reshape(KINDS * CLUSTERS, KINDS * EXPERTS).astype(jnp.bfloat16)
    spread = jnp.einsum("lm,ce->elmc", jnp.eye(TILES), belongs.astype(jnp.float32))
    spread = spread.reshape(EXPERTS * TILES, TILES * CLUSTERS).astype(jnp.bfloat16)

    anywhere = pl.BlockSpec(memory_space=pl.ANY)
    answer = pl.pallas_call(
        merge_kernel, out_shape=PACKED, in_specs=[whole] * 4 + [anywhere] * 10, out_specs=whole,
        scratch_shapes=[
            pltpu.VMEM((EXPERTS, BLOCK, D), jnp.bfloat16),
            pltpu.VMEM((EXPERTS, BLOCK, D), jnp.bfloat16),
            pltpu.VMEM((KINDS * EXPERTS, D), jnp.bfloat16),
            pltpu.VMEM((KINDS * EXPERTS, EXPERTS * BLOCK), jnp.bfloat16),
            pltpu.VMEM((KINDS * CLUSTERS, D), jnp.bfloat16),
            pltpu.SemaphoreType.DMA((20,)),
        ],
        compiler_params=params(), name="merge",
    )(received, share, members, spread, *pieces)
    returned = lax.all_to_all(answer, "expert", split_axis=0, concat_axis=0, tiled=True)
    part = jax.ShapeDtypeStruct((hidden, D), jnp.bfloat16)
    outs = pl.pallas_call(
        unpack_kernel, out_shape=(part,) * 3, in_specs=[whole], out_specs=(whole,) * 3,
        compiler_params=params(), name="unpack",
    )(returned)
    return tuple(o[None] for o in outs)


def solution(mesh):
    return jax.shard_map(
        body,
        mesh=mesh,
        in_specs=(
            P("expert", "dp"),
            P("expert", "dp"),
            P("expert", None),
            P("expert", None),
            P("expert", "dp", None),
            P("expert", "dp", None),
            P("expert", "dp", None),
            P(),
        ),
        out_specs=(P("expert", "dp", None), P("expert", "dp", None), P("expert", "dp", None)),
        check_vma=False,
    )
```

time: 536 us -> 454 us (0.85)
  other arithmetic: 54.1 us -> 5.4 us
  local copies, waits for them, and re-layouts: 63.1 us -> 18.5 us
  Pallas kernels: 0 us -> 38.7 us
  matrix products: 22.7 us -> 0 us
  between operations: 14.3 us -> 1.02 us
  starting transfers between devices: 61.4 us -> 73 us
    ppermute x0 -> x17, waiting for transfers between devices: none -> 197 us  [the longest x4 128 us: body(): lax.ppermute(block, 'expert', expert_pairs(lambda y, z: (y, z ^ bit)))]
    all_to_all x5 -> x1, waiting for transfers between devices: 134 us -> 0.01 us  [body(): lax.all_to_all(packed, 'expert', split_axis=0, concat_axis=0, tiled=True)]
    all_gather x2 -> x0, waiting for transfers between devices: 66.6 us -> none  [the longest x1 33.3 us: body(): lax.all_gather(recv_tok.reshape(rows_total, tokens.shape[1]), 'dp', axis=...]
    ppermute x0 -> x17, starting transfers between devices: none -> 54.1 us  [the longest x4 17.9 us: body(): lax.ppermute(block, 'expert', expert_pairs(lambda y, z: (y, z ^ bit)))]
    all_to_all x5 -> x1, starting transfers between devices: 61.1 us -> 18.9 us  [body(): lax.all_to_all(packed, 'expert', split_axis=0, concat_axis=0, tiled=True)]
    pallas_call x0 -> x3, Pallas kernels: none -> 38.7 us  [the longest x1 30.3 us: body(): pl.pallas_call(merge_kernel, out_shape=PACKED, in_specs=[whole] * 4 + [an...]
    unnamed x24 -> x22, local copies, waits for them, and re-layouts: 37.2 us -> 1.7 us
    unnamed x2 -> x1, other arithmetic: 31 us -> 0.08 us
  transfers between devices with their start and end apart: 7 -> 18, of which waited for: 5 -> 10; matrix products, arithmetic and copies ran while one was open for 14% -> 5% of each run, Pallas kernels for 0% -> 0%
where the time goes in v1:
time: 454 us; the launch traced here: 452 us
  waiting for transfers between devices  197 us (43%)
  blocking collectives  118 us (26%)
  starting transfers between devices  73 us (16%)
  Pallas kernels  38.7 us (9%)
  local copies, waits for them, and re-layouts  18.5 us (4%)
  other arithmetic  5.4 us (1%)
    ppermute x4, waiting for transfers between devices, body(): lax.ppermute(block, 'expert', expert_pairs(lambda y, z: (y, z ^ bit)))  128 us
    all_to_all x1, blocking collectives, body(): lax.all_to_all(answer, 'expert', split_axis=0, concat_axis=0, tiled=True)  118 us
    ppermute x2, waiting for transfers between devices, gather_ring(): before = lax.ppermute(value, axis, up)  51.5 us
    pallas_call x1, Pallas kernels, body(): pl.pallas_call(merge_kernel, out_shape=PACKED, in_specs=[whole] * 4 + [an...  30.3 us
    all_to_all x1, starting transfers between devices, body(): lax.all_to_all(packed, 'expert', split_axis=0, concat_axis=0, tiled=True)  18.9 us
    ppermute x4, starting transfers between devices, body(): lax.ppermute(block, 'expert', expert_pairs(lambda y, z: (y, z ^ bit)))  17.9 us
    ppermute x2, waiting for transfers between devices, gather_ring(): far_first = lax.ppermute(before[:half], axis, up)  13 us
    ppermute x5, starting transfers between devices, body(): pieces = near + tuple((lax.ppermute(piece, 'dp', across) for piece in near))  10.3 us
  transfers between devices with their start and end apart: 18, of which 10 were waited for; matrix products, arithmetic and copies ran while one was open for 5% of the time, Pallas kernels for 0%

profile of v1, /device:TPU:6, one launch (start us, length us, event | category | flops | bytes accessed | tf_op | source)
XLA Modules:
  0.0 452.4 jit_solution(13944488194097628396)
XLA Ops:
  0.6 4.4 pack.1
  5.1 18.9 %all-to-all-start = ((bf16[64,144,128]{2,1,0:T(8,128)(2,1)}), bf16[64,144,128]{2,1,0:T(8,128)(2,1)S(1)}, u32[]{:S(2)}, u32[]{:S(2)}) async-start(bf16[64,144,128]{2,1,0:T(8,128)(2,1)} %pack.1), calls=%async_computation | async-start | bytes 4718592 | tf_op jit(solution)/shard_map/all_to_all | solution.py:192
  24.0 0.0 copy-done.5
  24.0 0.1 copy.26
  24.1 0.0 copy-done.4
  24.1 0.1 copy.25
  24.1 0.2 select_reduce_fusion
  24.3 0.0 copy-done.2
  24.3 0.0 copy-done.3
  24.3 0.1 constant_dynamic-update-slice_fusion.4
  24.4 12.2 %collective-permute-start = (bf16[1,72,256]{2,1,0:T(8,128)(2,1)S(1)}, bf16[1,72,256]{2,1,0:T(8,128)(2,1)S(1)}, u32[]{:S(2)}, u32[]{:S(2)}) collective-permute-start(bf16[1,72,256]{2,1,0:T(8,128)(2,1)S(1)} %get-tuple-element.10), channel_id=1, source_target_pairs={{0,64},{8,72},{16,80},{24,88},{32,96},{40,104},{48,112},{56,120},{... | collective-permute-start | bytes 110600 | tf_op jit(solution)/shard_map/ppermute | solution.py:200
  36.6 101.5 %collective-permute-done = bf16[1,72,256]{2,1,0:T(8,128)(2,1)S(1)} collective-permute-done((bf16[1,72,256]{2,1,0:T(8,128)(2,1)S(1)}, bf16[1,72,256]{2,1,0:T(8,128)(2,1)S(1)}, u32[]{:S(2)}, u32[]{:S(2)}) %collective-permute-start) | collective-permute-done | bytes 36896 | tf_op jit(solution)/shard_map/ppermute | solution.py:200
  138.2 1.9 collective-permute-start.1
  140.1 9.5 %collective-permute-done.1 = bf16[2,72,256]{2,1,0:T(8,128)(2,1)S(1)} collective-permute-done((bf16[2,72,256]{2,1,0:T(8,128)(2,1)S(1)}, bf16[2,72,256]{2,1,0:T(8,128)(2,1)S(1)}, u32[]{:S(2)}, u32[]{:S(2)}) %collective-permute-start.1) | collective-permute-done | bytes 73760 | tf_op jit(solution)/shard_map/ppermute | solution.py:200
  149.6 1.9 collective-permute-start.2
  151.5 7.9 %collective-permute-done.2 = bf16[4,72,256]{2,1,0:T(8,128)(2,1)S(1)} collective-permute-done((bf16[4,72,256]{2,1,0:T(8,128)(2,1)S(1)}, bf16[4,72,256]{2,1,0:T(8,128)(2,1)S(1)}, u32[]{:S(2)}, u32[]{:S(2)}) %collective-permute-start.2) | collective-permute-done | bytes 147488 | tf_op jit(solution)/shard_map/ppermute | solution.py:200
  159.4 1.9 collective-permute-start.3
  161.4 8.8 %collective-permute-done.3 = bf16[8,72,256]{2,1,0:T(8,128)(2,1)S(1)} collective-permute-done((bf16[8,72,256]{2,1,0:T(8,128)(2,1)S(1)}, bf16[8,72,256]{2,1,0:T(8,128)(2,1)S(1)}, u32[]{:S(2)}, u32[]{:S(2)}) %collective-permute-start.3) | collective-permute-done | bytes 294944 | tf_op jit(solution)/shard_map/ppermute | solution.py:200
  170.3 3.0 collective-permute-start.4
  173.3 4.0 collective-permute-start.5
  177.4 10.4 %collective-permute-done.4 = bf16[16,72,256]{2,1,0:T(8,128)(2,1)S(1)} collective-permute-done((bf16[16,72,256]{2,1,0:T(8,128)(2,1)S(1)}, bf16[16,72,256]{2,1,0:T(8,128)(2,1)S(1)}, u32[]{:S(2)}, u32[]{:S(2)}) %collective-permute-start.4) | collective-permute-done | bytes 589856 | tf_op jit(solution)/shard_map/ppermute | solution.py:176
  187.8 1.9 collective-permute-start.6
  189.8 0.0 collective-permute-done.5
  189.8 5.1 %collective-permute-start.7 = (bf16[8,72,256]{2,1,0:T(8,128)(2,1)S(1)}, bf16[8,72,256]{2,1,0:T(8,128)(2,1)S(1)}, u32[]{:S(2)}, u32[]{:S(2)}) collective-permute-start(bf16[8,72,256]{2,1,0:T(8,128)(2,1)S(1)} %slice.45), channel_id=1, source_target_pairs={{0,384},{8,392},{16,400},{24,408},{32,416},{40,424},{48,432},{56,4... | collective-permute-start | bytes 884744 | tf_op jit(solution)/shard_map/ppermute | solution.py:179
  195.0 3.1 collective-permute-done.6
  198.2 1.2 collective-permute-done.7
  199.4 0.0 copy-start.1
  199.4 1.8 slice.47.refs_4_
  201.2 2.5 collective-permute-start.8
  203.8 3.5 collective-permute-start.9
  207.2 41.1 %collective-permute-done.8.refs_5_ = bf16[64,64,256]{2,1,0:T(8,128)(2,1)} collective-permute-done((bf16[64,64,256]{2,1,0:T(8,128)(2,1)}, bf16[64,64,256]{2,1,0:T(8,128)(2,1)}, u32[]{:S(2)}, u32[]{:S(2)}) %collective-permute-start.8) | collective-permute-done | bytes 2097184 | tf_op jit(solution)/shard_map/ppermute | solution.py:176
  248.3 1.3 slice.48
  249.6 0.0 copy-done.1
  249.6 3.6 collective-permute-start.10
  253.2 0.0 collective-permute-done.9.refs_6_
  253.2 1.3 slice.49
  254.5 2.3 collective-permute-start.11
  256.8 1.9 collective-permute-start.12
  258.7 2.4 collective-permute-start.13
  261.1 1.9 collective-permute-start.14
  263.1 9.9 %collective-permute-done.10.refs_7_ = bf16[32,64,256]{2,1,0:T(8,128)(2,1)} collective-permute-done((bf16[32,64,256]{2,1,0:T(8,128)(2,1)S(1)}, bf16[32,64,256]{2,1,0:T(8,128)(2,1)}, u32[]{:S(2)}, u32[]{:S(2)}) %collective-permute-start.10) | collective-permute-done | bytes 1048608 | tf_op jit(solution)/shard_map/ppermute | solution.py:178
  273.0 1.9 collective-permute-start.15
  274.9 3.9 collective-permute-done.11.refs_8_
  278.8 2.1 collective-permute-start.16
  280.9 0.1 copy.28
  281.0 0.2 fusion.1
  281.2 1.0 convert_element_type.41.refs_2_
  282.2 3.1 fusion
  285.3 6.2 %convert_element_type.44.refs_3_ = bf16[1024,256]{1,0:T(8,128)(2,1)} reshape(bf16[64,16,16,16]{3,2,1,0:T(8,128)(2,1)} %fusion) | data formatting | bytes 1048576 | tf_op jit(solution)/shard_map/convert_element_type | solution.py:221
  291.6 1.8 slice_convert_fusion
  293.3 1.5 reshape.20
  294.8 1.0 copy.27
  295.9 2.3 copy.29.refs_1_
  298.2 0.0 collective-permute-done.12.refs_9_
  298.2 0.0 collective-permute-done.13.refs_10_
  298.2 0.0 collective-permute-done.14.refs_11_
  298.2 0.0 collective-permute-done.15.refs_12_
  298.2 0.0 collective-permute-done.16.refs_13_
  298.2 0.0 all-to-all-done.refs_0_
  298.2 0.0 copy-start
  298.3 1.4 copy-done
  299.7 30.3 %merge.1 = bf16[64,144,128]{2,1,0:T(8,128)(2,1)} custom-call(bf16[64,144,128]{2,1,0:T(8,128)(2,1)} %copy-done, f32[64,2048]{1,0:T(8,128)} %copy.29.refs_1_, bf16[144,576]{1,0:T(8,128)(2,1)} %convert_element_type.41.refs_2_, bf16[1024,256]{1,0:T(8,128)(2,1)} %convert_element_type.44.refs_3_, bf16[64,64,256]{2,1,0:T(8,128)(2,1)} %slice.47.refs_4_, ...), custom_call_target="tpu_custom_call" | custom-call | tf_op jit(solution)/shard_map/merge/pallas_call | solution.py:224
  330.0 118.4 %all_to_all.10.packed = bf16[64,144,128]{2,1,0:T(8,128)(2,1)} all-to-all(bf16[64,144,128]{2,1,0:T(8,128)(2,1)} %merge.1), channel_id=1, replica_groups=mesh['expert'=64,'dp'=8] {'expert'}, dimensions={0} | all-to-all | bytes 4718592 | tf_op jit(solution)/shard_map/all_to_all | solution.py:236
  448.4 3.9 unpack.1
  (25 shorter events, 0.3 us)
Async XLA Ops:
  5.1 18.9 %copy-start.5 = (bf16[32,8]{0,1:T(8,128)(2,1)S(1)}, bf16[32,8]{0,1:T(8,128)(2,1)}, u32[]{:S(2)}) copy-start(bf16[32,8]{0,1:T(8,128)(2,1)} %param.11) | copy-start | bytes 1540
  5.1 19.0 %copy-start.4 = (s32[32,8]{0,1:T(8,128)S(1)}, s32[32,8]{0,1:T(8,128)}, u32[]{:S(2)}) copy-start(s32[32,8]{0,1:T(8,128)} %param.10) | copy-start | bytes 3076
  5.1 19.2 %copy-start.2 = (bf16[32,256]{1,0:T(8,128)(2,1)S(1)}, bf16[32,256]{1,0:T(8,128)(2,1)}, u32[]{:S(2)}) copy-start(bf16[32,256]{1,0:T(8,128)(2,1)} %param.9) | copy-start | bytes 49156
  5.1 19.2 %copy-start.3 = (bf16[32,256]{1,0:T(8,128)(2,1)S(1)}, bf16[32,256]{1,0:T(8,128)(2,1)}, u32[]{:S(2)}) copy-start(bf16[32,256]{1,0:T(8,128)(2,1)} %param.8) | copy-start | bytes 49156
  5.1 293.1 %all-to-all-start = ((bf16[64,144,128]{2,1,0:T(8,128)(2,1)}), bf16[64,144,128]{2,1,0:T(8,128)(2,1)S(1)}, u32[]{:S(2)}, u32[]{:S(2)}) async-start(bf16[64,144,128]{2,1,0:T(8,128)(2,1)} %pack.1), calls=%async_computation | async-start | bytes 4718592 | tf_op jit(solution)/shard_map/all_to_all | solution.py:192
  24.4 113.7 %collective-permute-start = (bf16[1,72,256]{2,1,0:T(8,128)(2,1)S(1)}, bf16[1,72,256]{2,1,0:T(8,128)(2,1)S(1)}, u32[]{:S(2)}, u32[]{:S(2)}) collective-permute-start(bf16[1,72,256]{2,1,0:T(8,128)(2,1)S(1)} %get-tuple-element.10), channel_id=1, source_target_pairs={{0,64},{8,72},{16,80},{24,88},{32,96},{40,104},{48,112},{56,120},{... | collective-permute-start | bytes 110600 | tf_op jit(solution)/shard_map/ppermute | solution.py:200
  138.2 11.4 %collective-permute-start.1 = (bf16[2,72,256]{2,1,0:T(8,128)(2,1)S(1)}, bf16[2,72,256]{2,1,0:T(8,128)(2,1)S(1)}, u32[]{:S(2)}, u32[]{:S(2)}) collective-permute-start(bf16[2,72,256]{2,1,0:T(8,128)(2,1)S(1)} %pad_maximum_fusion.2), channel_id=1, source_target_pairs={{0,32},{8,40},{16,48},{24,56},{32,0},{40,8},{48,16},{56,24},{64,96... | collective-permute-start | bytes 221192 | tf_op jit(solution)/shard_map/ppermute | solution.py:200
  149.6 9.9 %collective-permute-start.2 = (bf16[4,72,256]{2,1,0:T(8,128)(2,1)S(1)}, bf16[4,72,256]{2,1,0:T(8,128)(2,1)S(1)}, u32[]{:S(2)}, u32[]{:S(2)}) collective-permute-start(bf16[4,72,256]{2,1,0:T(8,128)(2,1)S(1)} %pad_maximum_fusion.1), channel_id=1, source_target_pairs={{0,16},{8,24},{16,0},{24,8},{32,48},{40,56},{48,32},{56,40},{64,80... | collective-permute-start | bytes 442376 | tf_op jit(solution)/shard_map/ppermute | solution.py:200
  159.4 10.8 %collective-permute-start.3 = (bf16[8,72,256]{2,1,0:T(8,128)(2,1)S(1)}, bf16[8,72,256]{2,1,0:T(8,128)(2,1)S(1)}, u32[]{:S(2)}, u32[]{:S(2)}) collective-permute-start(bf16[8,72,256]{2,1,0:T(8,128)(2,1)S(1)} %pad_maximum_fusion), channel_id=1, source_target_pairs={{0,8},{8,0},{16,24},{24,16},{32,40},{40,32},{48,56},{56,48},{64,72... | collective-permute-start | bytes 884744 | tf_op jit(solution)/shard_map/ppermute | solution.py:200
  170.3 17.5 %collective-permute-start.4 = (bf16[16,72,256]{2,1,0:T(8,128)(2,1)S(1)}, bf16[16,72,256]{2,1,0:T(8,128)(2,1)S(1)}, u32[]{:S(2)}, u32[]{:S(2)}) collective-permute-start(bf16[16,72,256]{2,1,0:T(8,128)(2,1)S(1)} %get-tuple-element.11), channel_id=1, source_target_pairs={{0,128},{8,136},{16,144},{24,152},{32,160},{40,168},{48,176},{56,1... | collective-permute-start | bytes 1769480 | tf_op jit(solution)/shard_map/ppermute | solution.py:176
  173.3 16.4 %collective-permute-start.5 = (bf16[16,72,256]{2,1,0:T(8,128)(2,1)S(1)}, bf16[16,72,256]{2,1,0:T(8,128)(2,1)S(1)}, u32[]{:S(2)}, u32[]{:S(2)}) collective-permute-start(bf16[16,72,256]{2,1,0:T(8,128)(2,1)S(1)} %get-tuple-element.11), channel_id=1, source_target_pairs={{0,384},{8,392},{16,400},{24,408},{32,416},{40,424},{48,432},{56,4... | collective-permute-start | bytes 1769480 | tf_op jit(solution)/shard_map/ppermute | solution.py:177
  187.8 10.3 %collective-permute-start.6 = (bf16[8,72,256]{2,1,0:T(8,128)(2,1)S(1)}, bf16[8,72,256]{2,1,0:T(8,128)(2,1)S(1)}, u32[]{:S(2)}, u32[]{:S(2)}) collective-permute-start(bf16[8,72,256]{2,1,0:T(8,128)(2,1)S(1)} %slice.44), channel_id=1, source_target_pairs={{0,128},{8,136},{16,144},{24,152},{32,160},{40,168},{48,176},{56,1... | collective-permute-start | bytes 884744 | tf_op jit(solution)/shard_map/ppermute | solution.py:178
  189.8 9.6 %collective-permute-start.7 = (bf16[8,72,256]{2,1,0:T(8,128)(2,1)S(1)}, bf16[8,72,256]{2,1,0:T(8,128)(2,1)S(1)}, u32[]{:S(2)}, u32[]{:S(2)}) collective-permute-start(bf16[8,72,256]{2,1,0:T(8,128)(2,1)S(1)} %slice.45), channel_id=1, source_target_pairs={{0,384},{8,392},{16,400},{24,408},{32,416},{40,424},{48,432},{56,4... | collective-permute-start | bytes 884744 | tf_op jit(solution)/shard_map/ppermute | solution.py:179
  199.4 50.2 %copy-start.1 = (bf16[64,72,256]{2,1,0:T(8,128)(2,1)}, bf16[64,72,256]{2,1,0:T(8,128)(2,1)S(1)}, u32[]{:S(2)}) copy-start(bf16[64,72,256]{2,1,0:T(8,128)(2,1)S(1)} %constant_dynamic-update-slice_fusion.5) | copy-start | bytes 7077892
  201.2 61.8 %copy-start.6 = (s32[64]{0:T(128)S(1)}, s32[64]{0:T(128)}, u32[]{:S(2)}) copy-start(s32[64]{0:T(128)} %param.15) | copy-start | bytes 772
  201.2 47.0 %collective-permute-start.8 = (bf16[64,64,256]{2,1,0:T(8,128)(2,1)}, bf16[64,64,256]{2,1,0:T(8,128)(2,1)}, u32[]{:S(2)}, u32[]{:S(2)}) collective-permute-start(bf16[64,64,256]{2,1,0:T(8,128)(2,1)} %slice.47.refs_4_), channel_id=1, source_target_pairs={{0,2},{1,3},{2,4},{3,5},{4,6},{5,7},{6,0},{7,1},{8,10},{9,11},{10,... | collective-permute-start | bytes 6291464 | tf_op jit(solution)/shard_map/ppermute | solution.py:176
  203.8 49.4 %collective-permute-start.9 = (bf16[64,64,256]{2,1,0:T(8,128)(2,1)}, bf16[64,64,256]{2,1,0:T(8,128)(2,1)}, u32[]{:S(2)}, u32[]{:S(2)}) collective-permute-start(bf16[64,64,256]{2,1,0:T(8,128)(2,1)} %slice.47.refs_4_), channel_id=1, source_target_pairs={{0,6},{1,7},{2,0},{3,1},{4,2},{5,3},{6,4},{7,5},{8,14},{9,15},{10,... | collective-permute-start | bytes 6291464 | tf_op jit(solution)/shard_map/ppermute | solution.py:177
  249.6 23.4 %collective-permute-start.10 = (bf16[32,64,256]{2,1,0:T(8,128)(2,1)S(1)}, bf16[32,64,256]{2,1,0:T(8,128)(2,1)}, u32[]{:S(2)}, u32[]{:S(2)}) collective-permute-start(bf16[32,64,256]{2,1,0:T(8,128)(2,1)S(1)} %slice.48), channel_id=1, source_target_pairs={{0,2},{1,3},{2,4},{3,5},{4,6},{5,7},{6,0},{7,1},{8,10},{9,11},{10,... | collective-permute-start | bytes 3145736 | tf_op jit(solution)/shard_map/ppermute | solution.py:178
  254.5 24.3 %collective-permute-start.11 = (bf16[32,64,256]{2,1,0:T(8,128)(2,1)S(1)}, bf16[32,64,256]{2,1,0:T(8,128)(2,1)}, u32[]{:S(2)}, u32[]{:S(2)}) collective-permute-start(bf16[32,64,256]{2,1,0:T(8,128)(2,1)S(1)} %slice.49), channel_id=1, source_target_pairs={{0,6},{1,7},{2,0},{3,1},{4,2},{5,3},{6,4},{7,5},{8,14},{9,15},{10,... | collective-permute-start | bytes 3145736 | tf_op jit(solution)/shard_map/ppermute | solution.py:179
  256.8 41.4 %collective-permute-start.12 = (bf16[64,64,256]{2,1,0:T(8,128)(2,1)}, bf16[64,64,256]{2,1,0:T(8,128)(2,1)}, u32[]{:S(2)}, u32[]{:S(2)}) collective-permute-start(bf16[64,64,256]{2,1,0:T(8,128)(2,1)} %slice.47.refs_4_), channel_id=1, source_target_pairs={{0,1},{1,0},{2,3},{3,2},{4,5},{5,4},{6,7},{7,6},{8,9},{9,8},{10,11... | collective-permute-start | bytes 6291464 | tf_op jit(solution)/shard_map/ppermute | solution.py:214
  258.7 39.5 %collective-permute-start.13 = (bf16[64,64,256]{2,1,0:T(8,128)(2,1)}, bf16[64,64,256]{2,1,0:T(8,128)(2,1)}, u32[]{:S(2)}, u32[]{:S(2)}) collective-permute-start(bf16[64,64,256]{2,1,0:T(8,128)(2,1)} %collective-permute-done.8.refs_5_), channel_id=1, source_target_pairs={{0,1},{1,0},{2,3},{3,2},{4,5},{5,4},{6,7},{7,6},{8,9},{9,8},{10,11... | collective-permute-start | bytes 6291464 | tf_op jit(solution)/shard_map/ppermute | solution.py:214
  261.1 37.1 %collective-permute-start.14 = (bf16[64,64,256]{2,1,0:T(8,128)(2,1)}, bf16[64,64,256]{2,1,0:T(8,128)(2,1)}, u32[]{:S(2)}, u32[]{:S(2)}) collective-permute-start(bf16[64,64,256]{2,1,0:T(8,128)(2,1)} %collective-permute-done.9.refs_6_), channel_id=1, source_target_pairs={{0,1},{1,0},{2,3},{3,2},{4,5},{5,4},{6,7},{7,6},{8,9},{9,8},{10,11... | collective-permute-start | bytes 6291464 | tf_op jit(solution)/shard_map/ppermute | solution.py:214
  273.0 25.2 %collective-permute-start.15 = (bf16[32,64,256]{2,1,0:T(8,128)(2,1)}, bf16[32,64,256]{2,1,0:T(8,128)(2,1)}, u32[]{:S(2)}, u32[]{:S(2)}) collective-permute-start(bf16[32,64,256]{2,1,0:T(8,128)(2,1)} %collective-permute-done.10.refs_7_), channel_id=1, source_target_pairs={{0,1},{1,0},{2,3},{3,2},{4,5},{5,4},{6,7},{7,6},{8,9},{9,8},{10,11... | collective-permute-start | bytes 3145736 | tf_op jit(solution)/shard_map/ppermute | solution.py:214
  278.8 19.4 %collective-permute-start.16 = (bf16[32,64,256]{2,1,0:T(8,128)(2,1)}, bf16[32,64,256]{2,1,0:T(8,128)(2,1)}, u32[]{:S(2)}, u32[]{:S(2)}) collective-permute-start(bf16[32,64,256]{2,1,0:T(8,128)(2,1)} %collective-permute-done.11.refs_8_), channel_id=1, source_target_pairs={{0,1},{1,0},{2,3},{3,2},{4,5},{5,4},{6,7},{7,6},{8,9},{9,8},{10,11... | collective-permute-start | bytes 3145736 | tf_op jit(solution)/shard_map/ppermute | solution.py:214
  298.2 1.5 copy-start

commit v2 on v1

v2 whole, which is shorter than its diff:
```python
import jax
import jax.numpy as jnp
from jax import lax
from jax.experimental import pallas as pl
from jax.experimental.pallas import tpu as pltpu
from jax.sharding import PartitionSpec as P

D = 2048
FF = 1536
MEMBERS = 4
EXPERTS = 64
CLUSTERS = 16
ROWS = 3
PARTS = ((0, 1, 2),)
LANES = 128
TILES = D // LANES
BLOCK = 32
WIDTH = 256
Y, Z = 4, 16
fisher_floor = 1e-06
VMEM_LIMIT = 60 * 1024 * 1024


def swap_matrix():
    row = lax.broadcasted_iota(jnp.int32, (256, 256), 0)
    col = lax.broadcasted_iota(jnp.int32, (256, 256), 1)
    hit = (row // 16 == col % 16) & (row % 16 == col // 16)
    return jnp.where(hit, 1.0, 0.0).astype(jnp.bfloat16)


def dot(left, right):
    return jnp.dot(left, right, preferred_element_type=jnp.float32)


def dot_t(left, right):
    return lax.dot_general(
        left, right, (((1,), (1,)), ((), ())), preferred_element_type=jnp.float32
    )


def picks(rows, cols, of_row):
    row = lax.broadcasted_iota(jnp.int32, (rows, cols), 0)
    col = lax.broadcasted_iota(jnp.int32, (rows, cols), 1)
    return jnp.where(of_row(row) == col, 1.0, 0.0).astype(jnp.bfloat16)


def member_table(belongs):
    shape = (belongs.shape[1] // EXPERTS * CLUSTERS, belongs.shape[1])
    filled = dot(picks(shape[0], CLUSTERS, lambda r: r % CLUSTERS), belongs)
    row = lax.broadcasted_iota(jnp.int32, shape, 0)
    col = lax.broadcasted_iota(jnp.int32, shape, 1)
    return jnp.where(row // CLUSTERS == col // EXPERTS, filled, 0.0).astype(jnp.bfloat16)


def spread_table(belongs):
    shape = (EXPERTS * TILES, TILES * CLUSTERS)
    filled = dot(picks(shape[0], EXPERTS, lambda r: r // TILES), belongs)
    row = lax.broadcasted_iota(jnp.int32, shape, 0)
    col = lax.broadcasted_iota(jnp.int32, shape, 1)
    return jnp.where(row % TILES == col // CLUSTERS, filled, 0.0).astype(jnp.bfloat16)


def parts_of():
    for part, groups in enumerate(PARTS):
        for m in range(3):
            for i, j in enumerate(groups):
                yield part, m * len(groups) + i, m, j


def pack_kernel(*refs):
    swap = swap_matrix()
    for part, q, m, j in parts_of():
        for kb in range(4):
            rows = slice(64 * j + 16 * kb, 64 * j + 16 * kb + 16)
            stacked = jnp.concatenate(
                [refs[m][rows, l * LANES : (l + 1) * LANES] for l in range(TILES)], axis=0
            )
            turned = dot(swap, stacked).astype(jnp.bfloat16)
            refs[3 + part][16 * kb : 16 * kb + 16, 16 * q : 16 * q + 16, :] = turned.reshape(
                16, 16, LANES
            )


def unpack_kernel(*refs):
    swap = swap_matrix()
    for part, q, m, j in parts_of():
        for kb in range(4):
            stacked = refs[part][16 * kb : 16 * kb + 16, 16 * q : 16 * q + 16, :]
            turned = dot(swap, stacked.reshape(256, LANES)).astype(jnp.bfloat16)
            rows = slice(64 * j + 16 * kb, 64 * j + 16 * kb + 16)
            for l in range(TILES):
                refs[len(PARTS) + m][rows, l * LANES : (l + 1) * LANES] = turned[
                    16 * l : 16 * l + 16
                ]


def merge_kernel(*refs):
    (packed, route_map, belongs_row, belongs_col) = refs[:4]
    pieces = refs[4:24]
    out, tok, cot, weights, fisher_rows, merged, sems = refs[24:]
    kinds = packed.shape[1] // TILES
    place = lax.axis_index("dp")
    x, core = place // 2, place % 2
    shifts = (0, 3, 1, 2)

    def bring(piece, target, first, shift, c, which, t):
        lane = pl.multiple_of((((x + shift) % 4) * 2 + c) * WIDTH, WIDTH)
        pltpu.make_async_copy(
            piece, target.at[first : first + piece.shape[0], :, pl.ds(lane, WIDTH)],
            sems.at[which, t],
        ).start()

    for t in range(8):
        for side in range(2):
            c = core if side == 0 else 1 - core
            tok_pieces = pieces[10 * side : 10 * side + 5]
            cot_pieces = pieces[10 * side + 5 : 10 * side + 10]
            for i in range(3):
                bring(tok_pieces[i].at[8 * t : 8 * t + 8], tok, 8 * t, shifts[i], c, 0, t)
            far = 8 * (t % 4)
            bring(tok_pieces[3 + t // 4].at[far : far + 8], tok, 8 * t, shifts[3], c, 0, t)
            for h in range(4):
                if t < 6:
                    piece, at = cot_pieces[t // 2], h
                else:
                    piece, at = cot_pieces[3 + h // 2], h % 2
                first = 16 * at + 8 * (t % 2)
                bring(piece.at[first : first + 8], cot, 8 * t, shifts[h], c, 1, t)

    def ready(t):
        for which, target in enumerate((tok, cot)):
            rows = target.at[8 * t : 8 * t + 8]
            pltpu.make_async_copy(rows, rows, sems.at[which, t]).wait()

    swap = swap_matrix()
    for q in range(kinds):
        for eb in range(4):
            stacked = packed[16 * eb : 16 * eb + 16, 16 * q : 16 * q + 16, :].reshape(256, LANES)
            turned = dot(swap, stacked).astype(jnp.bfloat16)
            rows = slice(64 * q + 16 * eb, 64 * q + 16 * eb + 16)
            for l in range(TILES):
                weights[rows, l * LANES : (l + 1) * LANES] = turned[16 * l : 16 * l + 16]
    third = kinds // 3 * EXPERTS
    table = member_table(belongs_row[...])

    def project(t):
        ready(t)
        at = 8 * t
        tok_rows = tok[pl.ds(at, 8)].reshape(256, D)
        cot_rows = cot[pl.ds(at, 8)].reshape(256, D)
        lane = 256 * t
        share = route_map[:, pl.ds(lane, 256)]
        share = jnp.concatenate([share] * (kinds // 3), axis=0)
        pre = dot_t(weights[0 : 2 * third, :], tok_rows) * (D**-0.5)
        act_grad = dot_t(weights[2 * third :, :], cot_rows) * (FF**-0.5) * share
        gate_pre, up_pre = pre[:third], pre[third:]
        sigmoid = jax.nn.sigmoid(gate_pre)
        silu = gate_pre * sigmoid
        slope = sigmoid * (1.0 + gate_pre * (1.0 - sigmoid))
        gate_grad = act_grad * up_pre * slope
        up_grad = act_grad * silu
        act = silu * up_pre * share
        for m, value in enumerate((gate_grad, up_grad, act)):
            fisher_rows[m * third : (m + 1) * third, pl.ds(lane, 256)] = (value * value).astype(
                jnp.bfloat16
            )

    for t in range(8):
        project(t)

    def merge(f):
        lane = f * WIDTH
        tok_cols = tok[:, :, pl.ds(lane, WIDTH)].reshape(2048, WIDTH)
        cot_cols = cot[:, :, pl.ds(lane, WIDTH)].reshape(2048, WIDTH)
        fisher_in = dot(fisher_rows[0 : 2 * third, :], tok_cols * tok_cols)
        fisher_down = dot(fisher_rows[2 * third :, :], cot_cols * cot_cols)
        fisher = jnp.concatenate(
            [fisher_in.astype(jnp.bfloat16), fisher_down.astype(jnp.bfloat16)], axis=0
        )
        product = fisher.astype(jnp.float32) * weights[:, pl.ds(lane, WIDTH)].astype(jnp.float32)
        high = product.astype(jnp.bfloat16)
        low = (product - high.astype(jnp.float32)).astype(jnp.bfloat16)
        numerator = dot(table, high) + dot(table, low)
        denominator = dot(table, fisher)
        merged[:, pl.ds(lane, WIDTH)] = (numerator / (denominator + fisher_floor)).astype(
            jnp.bfloat16
        )

    for f in range(8):
        merge(f)
    spread = spread_table(belongs_col[...])
    for q in range(kinds):
        stacked = jnp.concatenate(
            [merged[16 * q : 16 * q + 16, l * LANES : (l + 1) * LANES] for l in range(TILES)], axis=0
        )
        for eb in range(4):
            turned = dot(spread[256 * eb : 256 * eb + 256], stacked).astype(jnp.bfloat16)
            out[16 * eb : 16 * eb + 16, 16 * q : 16 * q + 16, :] = turned.reshape(16, 16, LANES)


def params():
    return pltpu.CompilerParams(vmem_limit_bytes=VMEM_LIMIT)


def packed_shape(kinds):
    return jax.ShapeDtypeStruct((EXPERTS, kinds * TILES, LANES), jnp.bfloat16)


def expert_pairs(move):
    return [(y * Z + z, move(y, z)[0] * Z + move(y, z)[1]) for y in range(Y) for z in range(Z)]


def dp_pairs(move):
    return [(2 * x + c, move(x, c)[0] * 2 + move(x, c)[1]) for x in range(4) for c in range(2)]


def gather_ring(value, axis, up, down):
    half = value.shape[0] // 2
    before = lax.ppermute(value, axis, up)
    after = lax.ppermute(value, axis, down)
    far_first = lax.ppermute(before[:half], axis, up)
    far_last = lax.ppermute(after[half:], axis, down)
    return value, before, after, far_first, far_last


def body(
    tokens, cotangent, routes, route_weights, gate_weight, up_weight, down_weight, cluster_order
):
    hidden = gate_weight.shape[1]
    whole = pl.BlockSpec(memory_space=pltpu.VMEM)
    shapes = tuple(packed_shape(3 * len(groups)) for groups in PARTS)
    packed = pl.pallas_call(
        pack_kernel, out_shape=shapes, in_specs=[whole] * 3, out_specs=(whole,) * len(PARTS),
        compiler_params=params(), name="pack",
    )(gate_weight[0], up_weight[0], down_weight[0])
    cluster = cluster_order // MEMBERS
    clusters = jnp.arange(CLUSTERS, dtype=jnp.int32)
    belongs_col = (cluster[:, None] == jnp.tile(clusters, TILES)[None, :]).astype(jnp.bfloat16)
    belongs_row = (clusters[:, None] == jnp.tile(cluster, 3 * ROWS)[None, :]).astype(jnp.bfloat16)

    chosen = routes[:, :, None] == jnp.arange(EXPERTS, dtype=jnp.int32)[None, None, :]
    share = jnp.sum(jnp.where(chosen, route_weights.astype(jnp.float32)[:, :, None], 0.0), axis=1)
    share = share.astype(jnp.bfloat16)
    share = jnp.concatenate([share[8 * i : 8 * i + 8] for i in range(4)], axis=1)
    block = jnp.concatenate([tokens, share, cotangent], axis=0)[None]

    def along_z(value, shift):
        return lax.ppermute(value, "expert", expert_pairs(lambda y, z: (y, (z + shift) % Z)))

    for moves in ((4, 8, 12), (1, -1, 2)):
        block = jnp.concatenate([block] + [along_z(block, shift) for shift in moves], axis=0)
    packed, block, belongs_row, belongs_col = lax.optimization_barrier(
        (packed, block, belongs_row, belongs_col)
    )

    def along_y(value):
        return gather_ring(
            value, "expert",
            expert_pairs(lambda y, z: ((y + 1) % Y, z)), expert_pairs(lambda y, z: ((y - 1) % Y, z)),
        )

    def along_x(value):
        return gather_ring(
            value, "dp",
            dp_pairs(lambda x, c: ((x + 1) % 4, c)), dp_pairs(lambda x, c: ((x - 1) % 4, c)),
        )

    received = []
    for part in packed:
        received.append(lax.all_to_all(part, "expert", split_axis=0, concat_axis=0, tiled=True))
    tok_block = jnp.concatenate(along_y(block[:, : BLOCK + 8]), axis=0)
    cot_block = jnp.concatenate(along_x(block[:, BLOCK + 8 :]), axis=0)
    share = tok_block[:, BLOCK:].reshape(EXPERTS, 8, 4, EXPERTS).transpose(3, 0, 2, 1)
    share = share.reshape(EXPERTS, EXPERTS * BLOCK).astype(jnp.float32)
    near = along_x(tok_block[:, :BLOCK]) + along_y(cot_block)
    across = dp_pairs(lambda x, c: (x, 1 - c))
    pieces = near + tuple(lax.ppermute(piece, "dp", across) for piece in near)

    anywhere = pl.BlockSpec(memory_space=pl.ANY)
    returned = []
    for n, part in enumerate(received):
        kinds = 3 * len(PARTS[n])
        answer = pl.pallas_call(
            merge_kernel, out_shape=shapes[n],
            in_specs=[whole] * 4 + [anywhere] * 20, out_specs=whole,
            scratch_shapes=[
                pltpu.VMEM((EXPERTS, BLOCK, D), jnp.bfloat16),
                pltpu.VMEM((EXPERTS, BLOCK, D), jnp.bfloat16),
                pltpu.VMEM((kinds * EXPERTS, D), jnp.bfloat16),
                pltpu.VMEM((kinds * EXPERTS, EXPERTS * BLOCK), jnp.bfloat16),
                pltpu.VMEM((kinds * CLUSTERS, D), jnp.bfloat16),
                pltpu.SemaphoreType.DMA((2, 8)),
            ],
            compiler_params=params(),
        )(part, share, belongs_row[:, : kinds * EXPERTS], belongs_col, *pieces)
        returned.append(lax.all_to_all(answer, "expert", split_axis=0, concat_axis=0, tiled=True))
    rows = jax.ShapeDtypeStruct((hidden, D), jnp.bfloat16)
    outs = pl.pallas_call(
        unpack_kernel, out_shape=(rows,) * 3, in_specs=[whole] * len(PARTS), out_specs=(whole,) * 3,
        compiler_params=params(), name="unpack",
    )(*returned)
    return tuple(o[None] for o in outs)


def solution(mesh):
    return jax.shard_map(
        body,
        mesh=mesh,
        in_specs=(
            P("expert", "dp"),
            P("expert", "dp"),
            P("expert", None),
            P("expert", None),
            P("expert", "dp", None),
            P("expert", "dp", None),
            P("expert", "dp", None),
            P(),
        ),
        out_specs=(P("expert", "dp", None), P("expert", "dp", None), P("expert", "dp", None)),
        check_vma=False,
    )
```

time: 454 us -> 358 us (0.79)
  waiting for transfers between devices: 197 us -> 59.3 us
  starting transfers between devices: 73 us -> 116 us
  blocking collectives: 118 us -> 128 us
  local copies, waits for them, and re-layouts: 18.5 us -> 11.7 us
  Pallas kernels: 38.7 us -> 33.7 us
    ppermute x4 -> x6, waiting for transfers between devices: 128 us -> 6.29 us  [along_z(): lax.ppermute(value, 'expert', expert_pairs(lambda y, z: (y, (z + shift) %...]
    ppermute x2 -> x4, waiting for transfers between devices: 51.5 us -> 0.01 us  [gather_ring(): before = lax.ppermute(value, axis, up)]
    ppermute x2 -> x4, waiting for transfers between devices: 0.01 us -> 35.5 us  [gather_ring(): after = lax.ppermute(value, axis, down)]
    ppermute x4 -> x6, starting transfers between devices: 17.9 us -> 34.9 us  [along_z(): lax.ppermute(value, 'expert', expert_pairs(lambda y, z: (y, (z + shift) %...]
    ppermute x5 -> x10, starting transfers between devices: 10.3 us -> 21.3 us  [body(): pieces = near + tuple((lax.ppermute(piece, 'dp', across) for piece in near))]
    all_to_all x1, starting transfers between devices: 18.9 us -> 8.03 us  [body(): lax.all_to_all(part, 'expert', split_axis=0, concat_axis=0, tiled=True)]
    all_to_all x1, blocking collectives: 118 us -> 128 us  [body(): lax.all_to_all(answer, 'expert', split_axis=0, concat_axis=0, tiled=True)]
    ppermute x2 -> x4, starting transfers between devices: 5.52 us -> 14.6 us  [gather_ring(): before = lax.ppermute(value, axis, up)]
  transfers between devices with their start and end apart: 18 -> 33, of which waited for: 10 -> 7; matrix products, arithmetic and copies ran while one was open for 5% -> 3% of each run, Pallas kernels for 0% -> 1%
where the time goes in v2:
time: 358 us; the launch traced here: 354 us
  blocking collectives  128 us (36%)
  starting transfers between devices  116 us (32%)
  waiting for transfers between devices  59.3 us (17%)
  Pallas kernels  33.7 us (9%)
  local copies, waits for them, and re-layouts  11.7 us (3%)
  other arithmetic  3.77 us (1%)
    all_to_all x1, blocking collectives, body(): lax.all_to_all(answer, 'expert', split_axis=0, concat_axis=0, tiled=True)  128 us
    ppermute x4, waiting for transfers between devices, gather_ring(): after = lax.ppermute(value, axis, down)  35.5 us
    ppermute x6, starting transfers between devices, along_z(): lax.ppermute(value, 'expert', expert_pairs(lambda y, z: (y, (z + shift) %...  34.9 us
    pallas_call x1, Pallas kernels, body(): pl.pallas_call(merge_kernel, out_shape=shapes[n], in_specs=[whole] * 4 +...  25.3 us
    ppermute x10, starting transfers between devices, body(): pieces = near + tuple((lax.ppermute(piece, 'dp', across) for piece in near))  21.3 us
    ppermute x4, starting transfers between devices, gather_ring(): before = lax.ppermute(value, axis, up)  14.6 us
    ppermute x4, starting transfers between devices, gather_ring(): far_first = lax.ppermute(before[:half], axis, up)  14.1 us
    ppermute x4, starting transfers between devices, gather_ring(): after = lax.ppermute(value, axis, down)  12.2 us
  transfers between devices with their start and end apart: 33, of which 7 were waited for; matrix products, arithmetic and copies ran while one was open for 3% of the time, Pallas kernels for 1%

profile of v2, /device:TPU:6, one launch (start us, length us, event | category | flops | bytes accessed | tf_op | source)
XLA Modules:
  0.0 354.4 jit_solution(17914250136325665346)
XLA Ops:
  0.6 0.8 copy.18
  1.4 0.8 copy.19
  2.1 0.2 select_reduce_fusion
  2.3 0.8 constant_dynamic-update-slice_fusion.6
  3.1 12.7 %collective-permute-start.2 = (bf16[1,72,256]{2,1,0:T(8,128)(2,1)S(1)}, bf16[1,72,256]{2,1,0:T(8,128)(2,1)S(1)}, u32[]{:S(2)}, u32[]{:S(2)}) collective-permute-start(bf16[1,72,256]{2,1,0:T(8,128)(2,1)S(1)} %get-tuple-element.18), channel_id=1, source_target_pairs={{0,96},{8,104},{16,112},{24,120},{32,0},{40,8},{48,16},{56,24},{64... | collective-permute-start | bytes 110600 | tf_op jit(solution)/shard_map/ppermute | solution.py:248
  15.9 4.9 %collective-permute-start.1 = (bf16[1,72,256]{2,1,0:T(8,128)(2,1)S(1)}, bf16[1,72,256]{2,1,0:T(8,128)(2,1)S(1)}, u32[]{:S(2)}, u32[]{:S(2)}) collective-permute-start(bf16[1,72,256]{2,1,0:T(8,128)(2,1)S(1)} %get-tuple-element.18), channel_id=1, source_target_pairs={{0,64},{8,72},{16,80},{24,88},{32,96},{40,104},{48,112},{56,120},{... | collective-permute-start | bytes 110600 | tf_op jit(solution)/shard_map/ppermute | solution.py:248
  20.8 7.8 %collective-permute-start = (bf16[1,72,256]{2,1,0:T(8,128)(2,1)S(1)}, bf16[1,72,256]{2,1,0:T(8,128)(2,1)S(1)}, u32[]{:S(2)}, u32[]{:S(2)}) collective-permute-start(bf16[1,72,256]{2,1,0:T(8,128)(2,1)S(1)} %get-tuple-element.18), channel_id=1, source_target_pairs={{0,32},{8,40},{16,48},{24,56},{32,64},{40,72},{48,80},{56,88},{64,... | collective-permute-start | bytes 110600 | tf_op jit(solution)/shard_map/ppermute | solution.py:248
  28.6 0.7 and_select_fusion
  29.3 0.1 eq.47
  29.4 0.1 eq.51
  29.4 0.7 compare_convert_fusion.refs_3_
  30.1 0.6 fusion.refs_2_
  30.7 4.4 %pack.1 = bf16[64,144,128]{2,1,0:T(8,128)(2,1)} custom-call(bf16[192,2048]{1,0:T(8,128)(2,1)} %bitcast.13, bf16[192,2048]{1,0:T(8,128)(2,1)} %bitcast.14, bf16[192,2048]{1,0:T(8,128)(2,1)} %bitcast.15), custom_call_target="tpu_custom_call" | custom-call | tf_op jit(solution)/shard_map/pack/pallas_call | solution.py:232
  35.2 3.4 collective-permute-start.5
  38.6 4.1 %collective-permute-start.4 = (bf16[4,72,256]{2,1,0:T(8,128)(2,1)S(1)}, bf16[4,72,256]{2,1,0:T(8,128)(2,1)S(1)}, u32[]{:S(2)}, u32[]{:S(2)}) collective-permute-start(bf16[4,72,256]{2,1,0:T(8,128)(2,1)S(1)} %pad_maximum_fusion), channel_id=1, source_target_pairs={{0,120},{8,0},{16,8},{24,16},{32,24},{40,32},{48,40},{56,48},{64,5... | collective-permute-start | bytes 442376 | tf_op jit(solution)/shard_map/ppermute | solution.py:248
  42.7 1.9 collective-permute-start.3
  44.7 6.3 %collective-permute-done.3 = bf16[4,72,256]{2,1,0:T(8,128)(2,1)S(1)} collective-permute-done((bf16[4,72,256]{2,1,0:T(8,128)(2,1)S(1)}, bf16[4,72,256]{2,1,0:T(8,128)(2,1)S(1)}, u32[]{:S(2)}, u32[]{:S(2)}) %collective-permute-start.3) | collective-permute-done | bytes 147488 | tf_op jit(solution)/shard_map/ppermute | solution.py:248
  51.0 8.0 %all-to-all-start = ((bf16[64,144,128]{2,1,0:T(8,128)(2,1)}), bf16[64,144,128]{2,1,0:T(8,128)(2,1)S(1)}, u32[]{:S(2)}, u32[]{:S(2)}) async-start(bf16[64,144,128]{2,1,0:T(8,128)(2,1)} %pack.1), calls=%async_computation | async-start | bytes 4718592 | tf_op jit(solution)/shard_map/all_to_all | solution.py:270
  59.1 2.7 collective-permute-start.15
  61.9 4.3 %collective-permute-start.14 = (bf16[16,32,256]{2,1,0:T(8,128)(2,1)S(1)}, bf16[16,32,256]{2,1,0:T(8,128)(2,1)S(1)}, u32[]{:S(2)}, u32[]{:S(2)}) collective-permute-start(bf16[16,32,256]{2,1,0:T(8,128)(2,1)S(1)} %get-tuple-element.19), channel_id=1, source_target_pairs={{0,2},{1,3},{2,4},{3,5},{4,6},{5,7},{6,0},{7,1},{8,10},{9,11},{10,... | collective-permute-start | bytes 786440 | tf_op jit(solution)/shard_map/ppermute | solution.py:219
  66.2 2.4 collective-permute-done.15
  68.6 1.9 collective-permute-start.17
  70.6 5.1 %collective-permute-start.16 = (bf16[8,32,256]{2,1,0:T(8,128)(2,1)S(1)}, bf16[8,32,256]{2,1,0:T(8,128)(2,1)S(1)}, u32[]{:S(2)}, u32[]{:S(2)}) collective-permute-start(bf16[8,32,256]{2,1,0:T(8,128)(2,1)S(1)} %slice.74), channel_id=1, source_target_pairs={{0,2},{1,3},{2,4},{3,5},{4,6},{5,7},{6,0},{7,1},{8,10},{9,11},{10,... | collective-permute-start | bytes 393224 | tf_op jit(solution)/shard_map/ppermute | solution.py:221
  75.8 2.4 collective-permute-done.16
  78.3 4.9 %collective-permute-start.19 = (bf16[64,32,256]{2,1,0:T(8,128)(2,1)S(1)}, bf16[64,32,256]{2,1,0:T(8,128)(2,1)S(1)}, u32[]{:S(2)}, u32[]{:S(2)}) collective-permute-start(bf16[64,32,256]{2,1,0:T(8,128)(2,1)S(1)} %constant_dynamic-update-slice_fusion.12.refs_9_), channel_id=1, source_target_pairs={{0,384},{8,392},{16,400},{24,408},{32,416},{40,424},{48,432},{56,4... | collective-permute-start | bytes 3145736 | tf_op jit(solution)/shard_map/ppermute | solution.py:220
  83.2 2.7 collective-permute-start.7
  85.9 3.2 collective-permute-start.6
  89.1 1.9 collective-permute-start.18
  91.0 24.4 %collective-permute-done.7 = bf16[16,40,256]{2,1,0:T(8,128)(2,1)S(1)} collective-permute-done((bf16[16,40,256]{2,1,0:T(8,128)(2,1)S(1)}, bf16[16,40,256]{2,1,0:T(8,128)(2,1)S(1)}, u32[]{:S(2)}, u32[]{:S(2)}) %collective-permute-start.7) | collective-permute-done | bytes 327712 | tf_op jit(solution)/shard_map/ppermute | solution.py:220
  115.5 5.6 %collective-permute-start.9 = (bf16[8,40,256]{2,1,0:T(8,128)(2,1)S(1)}, bf16[8,40,256]{2,1,0:T(8,128)(2,1)S(1)}, u32[]{:S(2)}, u32[]{:S(2)}) collective-permute-start(bf16[8,40,256]{2,1,0:T(8,128)(2,1)S(1)} %slice.69), channel_id=1, source_target_pairs={{0,384},{8,392},{16,400},{24,408},{32,416},{40,424},{48,432},{56,4... | collective-permute-start | bytes 491528 | tf_op jit(solution)/shard_map/ppermute | solution.py:222
  121.1 1.9 collective-permute-start.8
  123.1 8.9 %collective-permute-done.8 = bf16[8,40,256]{2,1,0:T(8,128)(2,1)S(1)} collective-permute-done((bf16[8,40,256]{2,1,0:T(8,128)(2,1)S(1)}, bf16[8,40,256]{2,1,0:T(8,128)(2,1)S(1)}, u32[]{:S(2)}, u32[]{:S(2)}) %collective-permute-start.8) | collective-permute-done | bytes 163872 | tf_op jit(solution)/shard_map/ppermute | solution.py:221
  132.1 0.1 slice.71.refs_4_
  132.2 1.9 collective-permute-start.11
  134.2 5.1 %collective-permute-start.10 = (bf16[64,32,256]{2,1,0:T(8,128)(2,1)S(1)}, bf16[64,32,256]{2,1,0:T(8,128)(2,1)}, u32[]{:S(2)}, u32[]{:S(2)}) collective-permute-start(bf16[64,32,256]{2,1,0:T(8,128)(2,1)S(1)} %slice.71.refs_4_), channel_id=1, source_target_pairs={{0,2},{1,3},{2,4},{3,5},{4,6},{5,7},{6,0},{7,1},{8,10},{9,11},{10,... | collective-permute-start | bytes 3145736 | tf_op jit(solution)/shard_map/ppermute | solution.py:219
  139.3 1.9 collective-permute-start.27
  141.3 2.4 collective-permute-start.22
  143.7 1.9 collective-permute-start.21
  145.7 1.1 slice.76
  146.7 8.7 %collective-permute-done.11.refs_6_ = bf16[64,32,256]{2,1,0:T(8,128)(2,1)} collective-permute-done((bf16[64,32,256]{2,1,0:T(8,128)(2,1)S(1)}, bf16[64,32,256]{2,1,0:T(8,128)(2,1)}, u32[]{:S(2)}, u32[]{:S(2)}) %collective-permute-start.11) | collective-permute-done | bytes 1048608 | tf_op jit(solution)/shard_map/ppermute | solution.py:220
  155.4 1.9 collective-permute-start.20
  157.3 1.1 slice.73
  158.4 1.9 collective-permute-start.29
  160.4 1.1 slice.72
  161.5 1.9 collective-permute-start.13
  163.4 5.1 %collective-permute-start.12 = (bf16[32,32,256]{2,1,0:T(8,128)(2,1)S(1)}, bf16[32,32,256]{2,1,0:T(8,128)(2,1)}, u32[]{:S(2)}, u32[]{:S(2)}) collective-permute-start(bf16[32,32,256]{2,1,0:T(8,128)(2,1)S(1)} %slice.72), channel_id=1, source_target_pairs={{0,2},{1,3},{2,4},{3,5},{4,6},{5,7},{6,0},{7,1},{8,10},{9,11},{10,... | collective-permute-start | bytes 1572872 | tf_op jit(solution)/shard_map/ppermute | solution.py:221
  168.6 0.0 copy-start.7
  168.6 1.9 collective-permute-start.31
  170.5 0.0 copy-start.8
  170.5 2.4 collective-permute-start.28
  173.0 6.1 %collective-permute-done.13.refs_8_ = bf16[32,32,256]{2,1,0:T(8,128)(2,1)} collective-permute-done((bf16[32,32,256]{2,1,0:T(8,128)(2,1)S(1)}, bf16[32,32,256]{2,1,0:T(8,128)(2,1)}, u32[]{:S(2)}, u32[]{:S(2)}) %collective-permute-start.13) | collective-permute-done | bytes 524320 | tf_op jit(solution)/shard_map/ppermute | solution.py:222
  179.0 1.9 collective-permute-start.30
  180.9 2.4 collective-permute-start.24
  183.4 1.9 collective-permute-start.23
  185.3 2.4 collective-permute-start.26
  187.8 2.1 collective-permute-start.25
  189.9 0.8 slice_convert_fusion
  190.8 1.5 reshape.19
  192.3 1.1 copy.20
  193.3 2.3 copy.21.refs_1_
  195.7 1.4 copy-done
  197.1 25.3 %shard_map.103 = bf16[64,144,128]{2,1,0:T(8,128)(2,1)} custom-call(bf16[64,144,128]{2,1,0:T(8,128)(2,1)} %copy-done, f32[64,2048]{1,0:T(8,128)} %copy.21.refs_1_, bf16[16,576]{1,0:T(8,128)(2,1)} %fusion.refs_2_, bf16[64,256]{1,0:T(8,128)(2,1)} %compare_convert_fusion.refs_3_, bf16[64,32,256]{2,1,0:T(8,128)(2,1)} %copy-done.1, ...), custom_call_target="tpu_custom_call" | custom-call | tf_op jit(solution)/shard_map/pallas_call | solution.py:283
  222.4 128.1 %all_to_all.10.refs_0_ = bf16[64,144,128]{2,1,0:T(8,128)(2,1)} all-to-all(bf16[64,144,128]{2,1,0:T(8,128)(2,1)} %shard_map.103), channel_id=1, replica_groups=mesh['expert'=64,'dp'=8] {'expert'}, dimensions={0} | all-to-all | bytes 4718592 | tf_op jit(solution)/shard_map/all_to_all | solution.py:296
  350.5 3.9 %unpack.1 = (bf16[192,2048]{1,0:T(8,128)(2,1)}, bf16[192,2048]{1,0:T(8,128)(2,1)}, bf16[192,2048]{1,0:T(8,128)(2,1)}) custom-call(bf16[64,144,128]{2,1,0:T(8,128)(2,1)} %all_to_all.10.refs_0_), custom_call_target="tpu_custom_call" | custom-call | tf_op jit(solution)/shard_map/unpack/pallas_call | solution.py:298
  (70 shorter events, 0.5 us)
Async XLA Ops:
  3.1 32.0 %collective-permute-start.2 = (bf16[1,72,256]{2,1,0:T(8,128)(2,1)S(1)}, bf16[1,72,256]{2,1,0:T(8,128)(2,1)S(1)}, u32[]{:S(2)}, u32[]{:S(2)}) collective-permute-start(bf16[1,72,256]{2,1,0:T(8,128)(2,1)S(1)} %get-tuple-element.18), channel_id=1, source_target_pairs={{0,96},{8,104},{16,112},{24,120},{32,0},{40,8},{48,16},{56,24},{64... | collective-permute-start | bytes 110600 | tf_op jit(solution)/shard_map/ppermute | solution.py:248
  15.9 19.3 %collective-permute-start.1 = (bf16[1,72,256]{2,1,0:T(8,128)(2,1)S(1)}, bf16[1,72,256]{2,1,0:T(8,128)(2,1)S(1)}, u32[]{:S(2)}, u32[]{:S(2)}) collective-permute-start(bf16[1,72,256]{2,1,0:T(8,128)(2,1)S(1)} %get-tuple-element.18), channel_id=1, source_target_pairs={{0,64},{8,72},{16,80},{24,88},{32,96},{40,104},{48,112},{56,120},{... | collective-permute-start | bytes 110600 | tf_op jit(solution)/shard_map/ppermute | solution.py:248
  20.8 14.4 %collective-permute-start = (bf16[1,72,256]{2,1,0:T(8,128)(2,1)S(1)}, bf16[1,72,256]{2,1,0:T(8,128)(2,1)S(1)}, u32[]{:S(2)}, u32[]{:S(2)}) collective-permute-start(bf16[1,72,256]{2,1,0:T(8,128)(2,1)S(1)} %get-tuple-element.18), channel_id=1, source_target_pairs={{0,32},{8,40},{16,48},{24,56},{32,64},{40,72},{48,80},{56,88},{64,... | collective-permute-start | bytes 110600 | tf_op jit(solution)/shard_map/ppermute | solution.py:248
  35.2 15.8 %collective-permute-start.5 = (bf16[4,72,256]{2,1,0:T(8,128)(2,1)S(1)}, bf16[4,72,256]{2,1,0:T(8,128)(2,1)S(1)}, u32[]{:S(2)}, u32[]{:S(2)}) collective-permute-start(bf16[4,72,256]{2,1,0:T(8,128)(2,1)S(1)} %pad_maximum_fusion), channel_id=1, source_target_pairs={{0,16},{8,24},{16,32},{24,40},{32,48},{40,56},{48,64},{56,72},{64,... | collective-permute-start | bytes 442376 | tf_op jit(solution)/shard_map/ppermute | solution.py:248
  38.6 12.4 %collective-permute-start.4 = (bf16[4,72,256]{2,1,0:T(8,128)(2,1)S(1)}, bf16[4,72,256]{2,1,0:T(8,128)(2,1)S(1)}, u32[]{:S(2)}, u32[]{:S(2)}) collective-permute-start(bf16[4,72,256]{2,1,0:T(8,128)(2,1)S(1)} %pad_maximum_fusion), channel_id=1, source_target_pairs={{0,120},{8,0},{16,8},{24,16},{32,24},{40,32},{48,40},{56,48},{64,5... | collective-permute-start | bytes 442376 | tf_op jit(solution)/shard_map/ppermute | solution.py:248
  42.7 8.2 %collective-permute-start.3 = (bf16[4,72,256]{2,1,0:T(8,128)(2,1)S(1)}, bf16[4,72,256]{2,1,0:T(8,128)(2,1)S(1)}, u32[]{:S(2)}, u32[]{:S(2)}) collective-permute-start(bf16[4,72,256]{2,1,0:T(8,128)(2,1)S(1)} %pad_maximum_fusion), channel_id=1, source_target_pairs={{0,8},{8,16},{16,24},{24,32},{32,40},{40,48},{48,56},{56,64},{64,7... | collective-permute-start | bytes 442376 | tf_op jit(solution)/shard_map/ppermute | solution.py:248
  51.0 144.6 %all-to-all-start = ((bf16[64,144,128]{2,1,0:T(8,128)(2,1)}), bf16[64,144,128]{2,1,0:T(8,128)(2,1)S(1)}, u32[]{:S(2)}, u32[]{:S(2)}) async-start(bf16[64,144,128]{2,1,0:T(8,128)(2,1)} %pack.1), calls=%async_computation | async-start | bytes 4718592 | tf_op jit(solution)/shard_map/all_to_all | solution.py:270
  59.1 9.5 %collective-permute-start.15 = (bf16[16,32,256]{2,1,0:T(8,128)(2,1)S(1)}, bf16[16,32,256]{2,1,0:T(8,128)(2,1)S(1)}, u32[]{:S(2)}, u32[]{:S(2)}) collective-permute-start(bf16[16,32,256]{2,1,0:T(8,128)(2,1)S(1)} %get-tuple-element.19), channel_id=1, source_target_pairs={{0,6},{1,7},{2,0},{3,1},{4,2},{5,3},{6,4},{7,5},{8,14},{9,15},{10,... | collective-permute-start | bytes 786440 | tf_op jit(solution)/shard_map/ppermute | solution.py:220
  61.9 8.7 %collective-permute-start.14 = (bf16[16,32,256]{2,1,0:T(8,128)(2,1)S(1)}, bf16[16,32,256]{2,1,0:T(8,128)(2,1)S(1)}, u32[]{:S(2)}, u32[]{:S(2)}) collective-permute-start(bf16[16,32,256]{2,1,0:T(8,128)(2,1)S(1)} %get-tuple-element.19), channel_id=1, source_target_pairs={{0,2},{1,3},{2,4},{3,5},{4,6},{5,7},{6,0},{7,1},{8,10},{9,11},{10,... | collective-permute-start | bytes 786440 | tf_op jit(solution)/shard_map/ppermute | solution.py:219
  68.6 9.6 %collective-permute-start.17 = (bf16[8,32,256]{2,1,0:T(8,128)(2,1)S(1)}, bf16[8,32,256]{2,1,0:T(8,128)(2,1)S(1)}, u32[]{:S(2)}, u32[]{:S(2)}) collective-permute-start(bf16[8,32,256]{2,1,0:T(8,128)(2,1)S(1)} %slice.75), channel_id=1, source_target_pairs={{0,6},{1,7},{2,0},{3,1},{4,2},{5,3},{6,4},{7,5},{8,14},{9,15},{10,... | collective-permute-start | bytes 393224 | tf_op jit(solution)/shard_map/ppermute | solution.py:222
  70.6 7.6 %collective-permute-start.16 = (bf16[8,32,256]{2,1,0:T(8,128)(2,1)S(1)}, bf16[8,32,256]{2,1,0:T(8,128)(2,1)S(1)}, u32[]{:S(2)}, u32[]{:S(2)}) collective-permute-start(bf16[8,32,256]{2,1,0:T(8,128)(2,1)S(1)} %slice.74), channel_id=1, source_target_pairs={{0,2},{1,3},{2,4},{3,5},{4,6},{5,7},{6,0},{7,1},{8,10},{9,11},{10,... | collective-permute-start | bytes 393224 | tf_op jit(solution)/shard_map/ppermute | solution.py:221
  78.3 61.1 %copy-start.3 = (bf16[64,32,256]{2,1,0:T(8,128)(2,1)}, bf16[64,32,256]{2,1,0:T(8,128)(2,1)S(1)}, u32[]{:S(2)}) copy-start(bf16[64,32,256]{2,1,0:T(8,128)(2,1)S(1)} %constant_dynamic-update-slice_fusion.12.refs_9_) | copy-start | bytes 3145732
  78.3 63.0 %collective-permute-start.19 = (bf16[64,32,256]{2,1,0:T(8,128)(2,1)S(1)}, bf16[64,32,256]{2,1,0:T(8,128)(2,1)S(1)}, u32[]{:S(2)}, u32[]{:S(2)}) collective-permute-start(bf16[64,32,256]{2,1,0:T(8,128)(2,1)S(1)} %constant_dynamic-update-slice_fusion.12.refs_9_), channel_id=1, source_target_pairs={{0,384},{8,392},{16,400},{24,408},{32,416},{40,424},{48,432},{56,4... | collective-permute-start | bytes 3145736 | tf_op jit(solution)/shard_map/ppermute | solution.py:220
  83.2 32.2 %collective-permute-start.7 = (bf16[16,40,256]{2,1,0:T(8,128)(2,1)S(1)}, bf16[16,40,256]{2,1,0:T(8,128)(2,1)S(1)}, u32[]{:S(2)}, u32[]{:S(2)}) collective-permute-start(bf16[16,40,256]{2,1,0:T(8,128)(2,1)S(1)} %get-tuple-element.21), channel_id=1, source_target_pairs={{0,384},{8,392},{16,400},{24,408},{32,416},{40,424},{48,432},{56,4... | collective-permute-start | bytes 983048 | tf_op jit(solution)/shard_map/ppermute | solution.py:220
  85.9 35.2 %collective-permute-start.6 = (bf16[16,40,256]{2,1,0:T(8,128)(2,1)S(1)}, bf16[16,40,256]{2,1,0:T(8,128)(2,1)S(1)}, u32[]{:S(2)}, u32[]{:S(2)}) collective-permute-start(bf16[16,40,256]{2,1,0:T(8,128)(2,1)S(1)} %get-tuple-element.21), channel_id=1, source_target_pairs={{0,128},{8,136},{16,144},{24,152},{32,160},{40,168},{48,176},{56,1... | collective-permute-start | bytes 983048 | tf_op jit(solution)/shard_map/ppermute | solution.py:219
  89.1 54.6 %collective-permute-start.18 = (bf16[64,32,256]{2,1,0:T(8,128)(2,1)S(1)}, bf16[64,32,256]{2,1,0:T(8,128)(2,1)}, u32[]{:S(2)}, u32[]{:S(2)}) collective-permute-start(bf16[64,32,256]{2,1,0:T(8,128)(2,1)S(1)} %constant_dynamic-update-slice_fusion.12.refs_9_), channel_id=1, source_target_pairs={{0,128},{8,136},{16,144},{24,152},{32,160},{40,168},{48,176},{56,1... | collective-permute-start | bytes 3145736 | tf_op jit(solution)/shard_map/ppermute | solution.py:219
  115.5 16.6 %collective-permute-start.9 = (bf16[8,40,256]{2,1,0:T(8,128)(2,1)S(1)}, bf16[8,40,256]{2,1,0:T(8,128)(2,1)S(1)}, u32[]{:S(2)}, u32[]{:S(2)}) collective-permute-start(bf16[8,40,256]{2,1,0:T(8,128)(2,1)S(1)} %slice.69), channel_id=1, source_target_pairs={{0,384},{8,392},{16,400},{24,408},{32,416},{40,424},{48,432},{56,4... | collective-permute-start | bytes 491528 | tf_op jit(solution)/shard_map/ppermute | solution.py:222
  121.1 10.9 %collective-permute-start.8 = (bf16[8,40,256]{2,1,0:T(8,128)(2,1)S(1)}, bf16[8,40,256]{2,1,0:T(8,128)(2,1)S(1)}, u32[]{:S(2)}, u32[]{:S(2)}) collective-permute-start(bf16[8,40,256]{2,1,0:T(8,128)(2,1)S(1)} %slice.68), channel_id=1, source_target_pairs={{0,128},{8,136},{16,144},{24,152},{32,160},{40,168},{48,176},{56,1... | collective-permute-start | bytes 491528 | tf_op jit(solution)/shard_map/ppermute | solution.py:221
  132.2 26.2 %copy-start.1 = (bf16[64,32,256]{2,1,0:T(8,128)(2,1)}, bf16[64,32,256]{2,1,0:T(8,128)(2,1)S(1)}, u32[]{:S(2)}) copy-start(bf16[64,32,256]{2,1,0:T(8,128)(2,1)S(1)} %slice.71.refs_4_) | copy-start | bytes 3145732
  132.2 23.2 %collective-permute-start.11 = (bf16[64,32,256]{2,1,0:T(8,128)(2,1)S(1)}, bf16[64,32,256]{2,1,0:T(8,128)(2,1)}, u32[]{:S(2)}, u32[]{:S(2)}) collective-permute-start(bf16[64,32,256]{2,1,0:T(8,128)(2,1)S(1)} %slice.71.refs_4_), channel_id=1, source_target_pairs={{0,6},{1,7},{2,0},{3,1},{4,2},{5,3},{6,4},{7,5},{8,14},{9,15},{10,... | collective-permute-start | bytes 3145736 | tf_op jit(solution)/shard_map/ppermute | solution.py:220
  134.2 24.3 %collective-permute-start.10 = (bf16[64,32,256]{2,1,0:T(8,128)(2,1)S(1)}, bf16[64,32,256]{2,1,0:T(8,128)(2,1)}, u32[]{:S(2)}, u32[]{:S(2)}) collective-permute-start(bf16[64,32,256]{2,1,0:T(8,128)(2,1)S(1)} %slice.71.refs_4_), channel_id=1, source_target_pairs={{0,2},{1,3},{2,4},{3,5},{4,6},{5,7},{6,0},{7,1},{8,10},{9,11},{10,... | collective-permute-start | bytes 3145736 | tf_op jit(solution)/shard_map/ppermute | solution.py:219
  139.3 22.1 %collective-permute-start.27 = (bf16[64,32,256]{2,1,0:T(8,128)(2,1)S(1)}, bf16[64,32,256]{2,1,0:T(8,128)(2,1)S(1)}, u32[]{:S(2)}, u32[]{:S(2)}) collective-permute-start(bf16[64,32,256]{2,1,0:T(8,128)(2,1)S(1)} %constant_dynamic-update-slice_fusion.12.refs_9_), channel_id=1, source_target_pairs={{0,1},{1,0},{2,3},{3,2},{4,5},{5,4},{6,7},{7,6},{8,9},{9,8},{10,11... | collective-permute-start | bytes 3145736 | tf_op jit(solution)/shard_map/ppermute | solution.py:277
  141.3 17.2 %copy-start.2 = (bf16[64,32,256]{2,1,0:T(8,128)(2,1)}, bf16[64,32,256]{2,1,0:T(8,128)(2,1)S(1)}, u32[]{:S(2)}) copy-start(bf16[64,32,256]{2,1,0:T(8,128)(2,1)S(1)} %collective-permute-done.19.refs_11_) | copy-start | bytes 3145732
  141.3 22.1 %collective-permute-start.22 = (bf16[64,32,256]{2,1,0:T(8,128)(2,1)S(1)}, bf16[64,32,256]{2,1,0:T(8,128)(2,1)S(1)}, u32[]{:S(2)}, u32[]{:S(2)}) collective-permute-start(bf16[64,32,256]{2,1,0:T(8,128)(2,1)S(1)} %slice.71.refs_4_), channel_id=1, source_target_pairs={{0,1},{1,0},{2,3},{3,2},{4,5},{5,4},{6,7},{7,6},{8,9},{9,8},{10,11... | collective-permute-start | bytes 3145736 | tf_op jit(solution)/shard_map/ppermute | solution.py:277
  143.7 24.8 %collective-permute-start.21 = (bf16[32,32,256]{2,1,0:T(8,128)(2,1)S(1)}, bf16[32,32,256]{2,1,0:T(8,128)(2,1)S(1)}, u32[]{:S(2)}, u32[]{:S(2)}) collective-permute-start(bf16[32,32,256]{2,1,0:T(8,128)(2,1)S(1)} %slice.77), channel_id=1, source_target_pairs={{0,384},{8,392},{16,400},{24,408},{32,416},{40,424},{48,432},{56,4... | collective-permute-start | bytes 1572872 | tf_op jit(solution)/shard_map/ppermute | solution.py:222
  155.4 15.1 %collective-permute-start.20 = (bf16[32,32,256]{2,1,0:T(8,128)(2,1)S(1)}, bf16[32,32,256]{2,1,0:T(8,128)(2,1)S(1)}, u32[]{:S(2)}, u32[]{:S(2)}) collective-permute-start(bf16[32,32,256]{2,1,0:T(8,128)(2,1)S(1)} %slice.76), channel_id=1, source_target_pairs={{0,128},{8,136},{16,144},{24,152},{32,160},{40,168},{48,176},{56,1... | collective-permute-start | bytes 1572872 | tf_op jit(solution)/shard_map/ppermute | solution.py:221
  158.4 26.9 %collective-permute-start.29 = (bf16[64,32,256]{2,1,0:T(8,128)(2,1)S(1)}, bf16[64,32,256]{2,1,0:T(8,128)(2,1)S(1)}, u32[]{:S(2)}, u32[]{:S(2)}) collective-permute-start(bf16[64,32,256]{2,1,0:T(8,128)(2,1)S(1)} %collective-permute-done.19.refs_11_), channel_id=1, source_target_pairs={{0,1},{1,0},{2,3},{3,2},{4,5},{5,4},{6,7},{7,6},{8,9},{9,8},{10,11... | collective-permute-start | bytes 3145736 | tf_op jit(solution)/shard_map/ppermute | solution.py:277
  161.5 28.4 %copy-start.4 = (bf16[64,32,256]{2,1,0:T(8,128)(2,1)}, bf16[64,32,256]{2,1,0:T(8,128)(2,1)S(1)}, u32[]{:S(2)}) copy-start(bf16[64,32,256]{2,1,0:T(8,128)(2,1)S(1)} %collective-permute-done.27.refs_19_) | copy-start | bytes 3145732
  161.5 17.5 %collective-permute-start.13 = (bf16[32,32,256]{2,1,0:T(8,128)(2,1)S(1)}, bf16[32,32,256]{2,1,0:T(8,128)(2,1)}, u32[]{:S(2)}, u32[]{:S(2)}) collective-permute-start(bf16[32,32,256]{2,1,0:T(8,128)(2,1)S(1)} %slice.73), channel_id=1, source_target_pairs={{0,6},{1,7},{2,0},{3,1},{4,2},{5,3},{6,4},{7,5},{8,14},{9,15},{10,... | collective-permute-start | bytes 1572872 | tf_op jit(solution)/shard_map/ppermute | solution.py:222
  163.4 26.5 %copy-start.5 = (bf16[64,32,256]{2,1,0:T(8,128)(2,1)}, bf16[64,32,256]{2,1,0:T(8,128)(2,1)S(1)}, u32[]{:S(2)}) copy-start(bf16[64,32,256]{2,1,0:T(8,128)(2,1)S(1)} %collective-permute-done.22.refs_14_) | copy-start | bytes 3145732
  163.4 17.5 %collective-permute-start.12 = (bf16[32,32,256]{2,1,0:T(8,128)(2,1)S(1)}, bf16[32,32,256]{2,1,0:T(8,128)(2,1)}, u32[]{:S(2)}, u32[]{:S(2)}) collective-permute-start(bf16[32,32,256]{2,1,0:T(8,128)(2,1)S(1)} %slice.72), channel_id=1, source_target_pairs={{0,2},{1,3},{2,4},{3,5},{4,6},{5,7},{6,0},{7,1},{8,10},{9,11},{10,... | collective-permute-start | bytes 1572872 | tf_op jit(solution)/shard_map/ppermute | solution.py:221
  168.6 21.3 %copy-start.7 = (bf16[32,32,256]{2,1,0:T(8,128)(2,1)}, bf16[32,32,256]{2,1,0:T(8,128)(2,1)S(1)}, u32[]{:S(2)}) copy-start(bf16[32,32,256]{2,1,0:T(8,128)(2,1)S(1)} %collective-permute-done.21.refs_13_) | copy-start | bytes 1572868
  168.6 14.8 %collective-permute-start.31 = (bf16[32,32,256]{2,1,0:T(8,128)(2,1)S(1)}, bf16[32,32,256]{2,1,0:T(8,128)(2,1)S(1)}, u32[]{:S(2)}, u32[]{:S(2)}) collective-permute-start(bf16[32,32,256]{2,1,0:T(8,128)(2,1)S(1)} %collective-permute-done.21.refs_13_), channel_id=1, source_target_pairs={{0,1},{1,0},{2,3},{3,2},{4,5},{5,4},{6,7},{7,6},{8,9},{9,8},{10,11... | collective-permute-start | bytes 1572872 | tf_op jit(solution)/shard_map/ppermute | solution.py:277
  170.5 19.4 %copy-start.8 = (bf16[32,32,256]{2,1,0:T(8,128)(2,1)}, bf16[32,32,256]{2,1,0:T(8,128)(2,1)S(1)}, u32[]{:S(2)}) copy-start(bf16[32,32,256]{2,1,0:T(8,128)(2,1)S(1)} %collective-permute-done.20.refs_12_) | copy-start | bytes 1572868
  170.5 25.1 %collective-permute-start.28 = (bf16[64,32,256]{2,1,0:T(8,128)(2,1)}, bf16[64,32,256]{2,1,0:T(8,128)(2,1)}, u32[]{:S(2)}, u32[]{:S(2)}) collective-permute-start(bf16[64,32,256]{2,1,0:T(8,128)(2,1)} %collective-permute-done.18.refs_10_), channel_id=1, source_target_pairs={{0,1},{1,0},{2,3},{3,2},{4,5},{5,4},{6,7},{7,6},{8,9},{9,8},{10,11... | collective-permute-start | bytes 3145736 | tf_op jit(solution)/shard_map/ppermute | solution.py:277
  179.0 8.7 %collective-permute-start.30 = (bf16[32,32,256]{2,1,0:T(8,128)(2,1)S(1)}, bf16[32,32,256]{2,1,0:T(8,128)(2,1)S(1)}, u32[]{:S(2)}, u32[]{:S(2)}) collective-permute-start(bf16[32,32,256]{2,1,0:T(8,128)(2,1)S(1)} %collective-permute-done.20.refs_12_), channel_id=1, source_target_pairs={{0,1},{1,0},{2,3},{3,2},{4,5},{5,4},{6,7},{7,6},{8,9},{9,8},{10,11... | collective-permute-start | bytes 1572872 | tf_op jit(solution)/shard_map/ppermute | solution.py:277
  180.9 14.7 %collective-permute-start.24 = (bf16[64,32,256]{2,1,0:T(8,128)(2,1)}, bf16[64,32,256]{2,1,0:T(8,128)(2,1)}, u32[]{:S(2)}, u32[]{:S(2)}) collective-permute-start(bf16[64,32,256]{2,1,0:T(8,128)(2,1)} %collective-permute-done.11.refs_6_), channel_id=1, source_target_pairs={{0,1},{1,0},{2,3},{3,2},{4,5},{5,4},{6,7},{7,6},{8,9},{9,8},{10,11... | collective-permute-start | bytes 3145736 | tf_op jit(solution)/shard_map/ppermute | solution.py:277
  183.4 6.5 %copy-start.9 = (bf16[32,32,256]{2,1,0:T(8,128)(2,1)}, bf16[32,32,256]{2,1,0:T(8,128)(2,1)S(1)}, u32[]{:S(2)}) copy-start(bf16[32,32,256]{2,1,0:T(8,128)(2,1)S(1)} %collective-permute-done.31.refs_23_) | copy-start | bytes 1572868
  183.4 12.3 %collective-permute-start.23 = (bf16[64,32,256]{2,1,0:T(8,128)(2,1)}, bf16[64,32,256]{2,1,0:T(8,128)(2,1)}, u32[]{:S(2)}, u32[]{:S(2)}) collective-permute-start(bf16[64,32,256]{2,1,0:T(8,128)(2,1)} %collective-permute-done.10.refs_5_), channel_id=1, source_target_pairs={{0,1},{1,0},{2,3},{3,2},{4,5},{5,4},{6,7},{7,6},{8,9},{9,8},{10,11... | collective-permute-start | bytes 3145736 | tf_op jit(solution)/shard_map/ppermute | solution.py:277
  185.3 4.6 %copy-start.6 = (bf16[64,32,256]{2,1,0:T(8,128)(2,1)}, bf16[64,32,256]{2,1,0:T(8,128)(2,1)S(1)}, u32[]{:S(2)}) copy-start(bf16[64,32,256]{2,1,0:T(8,128)(2,1)S(1)} %collective-permute-done.29.refs_21_) | copy-start | bytes 3145732
  185.3 10.3 %collective-permute-start.26 = (bf16[32,32,256]{2,1,0:T(8,128)(2,1)}, bf16[32,32,256]{2,1,0:T(8,128)(2,1)}, u32[]{:S(2)}, u32[]{:S(2)}) collective-permute-start(bf16[32,32,256]{2,1,0:T(8,128)(2,1)} %collective-permute-done.13.refs_8_), channel_id=1, source_target_pairs={{0,1},{1,0},{2,3},{3,2},{4,5},{5,4},{6,7},{7,6},{8,9},{9,8},{10,11... | collective-permute-start | bytes 1572872 | tf_op jit(solution)/shard_map/ppermute | solution.py:277
  187.8 2.2 copy-start.10
  187.8 7.9 %collective-permute-start.25 = (bf16[32,32,256]{2,1,0:T(8,128)(2,1)}, bf16[32,32,256]{2,1,0:T(8,128)(2,1)}, u32[]{:S(2)}, u32[]{:S(2)}) collective-permute-start(bf16[32,32,256]{2,1,0:T(8,128)(2,1)} %collective-permute-done.12.refs_7_), channel_id=1, source_target_pairs={{0,1},{1,0},{2,3},{3,2},{4,5},{5,4},{6,7},{7,6},{8,9},{9,8},{10,11... | collective-permute-start | bytes 1572872 | tf_op jit(solution)/shard_map/ppermute | solution.py:277
  195.7 1.4 copy-start

commit v3 on v2

--- a/solution.py
+++ b/solution.py
@@ -4,6 +4,7 @@
 from jax.experimental import pallas as pl
 from jax.experimental.pallas import tpu as pltpu
 from jax.sharding import PartitionSpec as P
+
 
 D = 2048
 FF = 1536
@@ -60,6 +61,15 @@
     return jnp.where(row % TILES == col // CLUSTERS, filled, 0.0).astype(jnp.bfloat16)
 
 
+def turn(left, blocks):
+    turned = []
+    for i in range(0, len(blocks), 2):
+        pair = blocks[i : i + 2]
+        both = dot(left, jnp.concatenate(pair, axis=1)).astype(jnp.bfloat16)
+        turned += [both[:, n * LANES : (n + 1) * LANES] for n in range(len(pair))]
+    return turned
+
+
 def parts_of():
     for part, groups in enumerate(PARTS):
         for m in range(3):
@@ -69,27 +79,31 @@
 
 def pack_kernel(*refs):
     swap = swap_matrix()
-    for part, q, m, j in parts_of():
-        for kb in range(4):
+    groups = list(parts_of())
+    for kb in range(4):
+        stacked = []
+        for _, _, m, j in groups:
             rows = slice(64 * j + 16 * kb, 64 * j + 16 * kb + 16)
-            stacked = jnp.concatenate(
-                [refs[m][rows, l * LANES : (l + 1) * LANES] for l in range(TILES)], axis=0
-            )
-            turned = dot(swap, stacked).astype(jnp.bfloat16)
-            refs[3 + part][16 * kb : 16 * kb + 16, 16 * q : 16 * q + 16, :] = turned.reshape(
+            tiles = [refs[m][rows, l * LANES : (l + 1) * LANES] for l in range(TILES)]
+            stacked.append(jnp.concatenate(tiles, axis=0))
+        for (part, q, _, _), block in zip(groups, turn(swap, stacked)):
+            refs[3 + part][16 * kb : 16 * kb + 16, 16 * q : 16 * q + 16, :] = block.reshape(
                 16, 16, LANES
             )
 
 
 def unpack_kernel(*refs):
     swap = swap_matrix()
-    for part, q, m, j in parts_of():
-        for kb in range(4):
-            stacked = refs[part][16 * kb : 16 * kb + 16, 16 * q : 16 * q + 16, :]
-            turned = dot(swap, stacked.reshape(256, LANES)).astype(jnp.bfloat16)
+    groups = list(parts_of())
+    for kb in range(4):
+        stacked = [
+            refs[part][16 * kb : 16 * kb + 16, 16 * q : 16 * q + 16, :].reshape(256, LANES)
+            for part, q, _, _ in groups
+        ]
+        for (_, _, m, j), block in zip(groups, turn(swap, stacked)):
             rows = slice(64 * j + 16 * kb, 64 * j + 16 * kb + 16)
             for l in range(TILES):
-                refs[len(PARTS) + m][rows, l * LANES : (l + 1) * LANES] = turned[
+                refs[len(PARTS) + m][rows, l * LANES : (l + 1) * LANES] = block[
                     16 * l : 16 * l + 16
                 ]
 
@@ -133,13 +147,15 @@
             pltpu.make_async_copy(rows, rows, sems.at[which, t]).wait()
 
     swap = swap_matrix()
-    for q in range(kinds):
-        for eb in range(4):
-            stacked = packed[16 * eb : 16 * eb + 16, 16 * q : 16 * q + 16, :].reshape(256, LANES)
-            turned = dot(swap, stacked).astype(jnp.bfloat16)
+    for eb in range(4):
+        stacked = [
+            packed[16 * eb : 16 * eb + 16, 16 * q : 16 * q + 16, :].reshape(256, LANES)
+            for q in range(kinds)
+        ]
+        for q, block in enumerate(turn(swap, stacked)):
             rows = slice(64 * q + 16 * eb, 64 * q + 16 * eb + 16)
             for l in range(TILES):
-                weights[rows, l * LANES : (l + 1) * LANES] = turned[16 * l : 16 * l + 16]
+                weights[rows, l * LANES : (l + 1) * LANES] = block[16 * l : 16 * l + 16]
     third = kinds // 3 * EXPERTS
     table = member_table(belongs_row[...])
 
@@ -178,10 +194,8 @@
             [fisher_in.astype(jnp.bfloat16), fisher_down.astype(jnp.bfloat16)], axis=0
         )
         product = fisher.astype(jnp.float32) * weights[:, pl.ds(lane, WIDTH)].astype(jnp.float32)
-        high = product.astype(jnp.bfloat16)
-        low = (product - high.astype(jnp.float32)).astype(jnp.bfloat16)
-        numerator = dot(table, high) + dot(table, low)
-        denominator = dot(table, fisher)
+        sums = dot(table, jnp.concatenate([product.astype(jnp.bfloat16), fisher], axis=1))
+        numerator, denominator = sums[:, :WIDTH], sums[:, WIDTH:]
         merged[:, pl.ds(lane, WIDTH)] = (numerator / (denominator + fisher_floor)).astype(
             jnp.bfloat16
         )
@@ -189,13 +203,15 @@
     for f in range(8):
         merge(f)
     spread = spread_table(belongs_col[...])
-    for q in range(kinds):
-        stacked = jnp.concatenate(
+    stacked = [
+        jnp.concatenate(
             [merged[16 * q : 16 * q + 16, l * LANES : (l + 1) * LANES] for l in range(TILES)], axis=0
         )
-        for eb in range(4):
-            turned = dot(spread[256 * eb : 256 * eb + 256], stacked).astype(jnp.bfloat16)
-            out[16 * eb : 16 * eb + 16, 16 * q : 16 * q + 16, :] = turned.reshape(16, 16, LANES)
+        for q in range(kinds)
+    ]
+    for eb in range(4):
+        for q, block in enumerate(turn(spread[256 * eb : 256 * eb + 256], stacked)):
+            out[16 * eb : 16 * eb + 16, 16 * q : 16 * q + 16, :] = block.reshape(16, 16, LANES)
 
 
 def params():
@@ -212,15 +228,6 @@
 
 def dp_pairs(move):
     return [(2 * x + c, move(x, c)[0] * 2 + move(x, c)[1]) for x in range(4) for c in range(2)]
-
-
-def gather_ring(value, axis, up, down):
-    half = value.shape[0] // 2
-    before = lax.ppermute(value, axis, up)
-    after = lax.ppermute(value, axis, down)
-    far_first = lax.ppermute(before[:half], axis, up)
-    far_last = lax.ppermute(after[half:], axis, down)
-    return value, before, after, far_first, far_last
 
 
 def body(
@@ -247,32 +254,39 @@
     def along_z(value, shift):
         return lax.ppermute(value, "expert", expert_pairs(lambda y, z: (y, (z + shift) % Z)))
 
-    for moves in ((4, 8, 12), (1, -1, 2)):
-        block = jnp.concatenate([block] + [along_z(block, shift) for shift in moves], axis=0)
+    block = jnp.concatenate([block] + [along_z(block, shift) for shift in (4, 8, 12)], axis=0)
     packed, block, belongs_row, belongs_col = lax.optimization_barrier(
         (packed, block, belongs_row, belongs_col)
     )
 
-    def along_y(value):
-        return gather_ring(
-            value, "expert",
-            expert_pairs(lambda y, z: ((y + 1) % Y, z)), expert_pairs(lambda y, z: ((y - 1) % Y, z)),
-        )
-
-    def along_x(value):
-        return gather_ring(
-            value, "dp",
-            dp_pairs(lambda x, c: ((x + 1) % 4, c)), dp_pairs(lambda x, c: ((x - 1) % 4, c)),
-        )
-
+    def along_y(value, shift):
+        return lax.ppermute(value, "expert", expert_pairs(lambda y, z: ((y + shift) % Y, z)))
+
+    def along_x(value, shift):
+        return lax.ppermute(value, "dp", dp_pairs(lambda x, c: ((x + shift) % 4, c)))
+
+    def whole_ring(value, along):
+        return jnp.concatenate([value] + [along(value, shift) for shift in (1, -1, 2)], axis=0)
+
+    def split_ring(value, along, beside=None):
+        half = value.shape[0] // 2
+        before, after = along(value, 1), along(value, -1)
+        if beside is not None:
+            before, after, beside = lax.optimization_barrier((before, after, beside))
+        return (value, before, after, along(before[:half], 1), along(after[half:], -1)), beside
+
+    near_z = [along_z(block, shift) for shift in (1, -1, 2)]
+    block = jnp.concatenate([block] + near_z, axis=0)
     received = []
     for part in packed:
         received.append(lax.all_to_all(part, "expert", split_axis=0, concat_axis=0, tiled=True))
-    tok_block = jnp.concatenate(along_y(block[:, : BLOCK + 8]), axis=0)
-    cot_block = jnp.concatenate(along_x(block[:, BLOCK + 8 :]), axis=0)
+    tok_block = whole_ring(block[:, : BLOCK + 8], along_y)
+    cot_block = whole_ring(block[:, BLOCK + 8 :], along_x)
     share = tok_block[:, BLOCK:].reshape(EXPERTS, 8, 4, EXPERTS).transpose(3, 0, 2, 1)
     share = share.reshape(EXPERTS, EXPERTS * BLOCK).astype(jnp.float32)
-    near = along_x(tok_block[:, :BLOCK]) + along_y(cot_block)
+    cot_near, _ = split_ring(cot_block, along_y)
+    tok_near, share = split_ring(tok_block[:, :BLOCK], along_x, share)
+    near = tok_near + cot_near
     across = dp_pairs(lambda x, c: (x, 1 - c))
     pieces = near + tuple(lax.ppermute(piece, "dp", across) for piece in near)
 

time: 358 us -> 446 us (1.25)
  waiting for transfers between devices: 59.3 us -> 149 us
    ppermute x6, waiting for transfers between devices: 6.29 us -> 99.5 us  [along_z(): lax.ppermute(value, 'expert', expert_pairs(lambda y, z: (y, (z + shift) %...]
    ppermute x16 -> x14, starting transfers between devices: 52.2 us -> 45 us  [the longest x7 24.5 us: along_x(): lax.ppermute(value, 'dp', dp_pairs(lambda x, c: ((x + shift) % 4, c)))]
    ppermute x16 -> x14, waiting for transfers between devices: 53 us -> 48.8 us  [the longest x7 28.5 us: along_y(): lax.ppermute(value, 'expert', expert_pairs(lambda y, z: ((y + shift) % Y,...]
  transfers between devices with their start and end apart: 33 -> 31, of which waited for: 7 -> 9; matrix products, arithmetic and copies ran while one was open for 3% -> 3% of each run, Pallas kernels for 1% -> 1%
where the time goes in v3:
time: 446 us; the launch traced here: 442 us
  waiting for transfers between devices  149 us (33%)
  blocking collectives  130 us (29%)
  starting transfers between devices  113 us (25%)
  Pallas kernels  31.5 us (7%)
  local copies, waits for them, and re-layouts  13.3 us (3%)
    all_to_all x1, blocking collectives, body(): lax.all_to_all(answer, 'expert', split_axis=0, concat_axis=0, tiled=True)  130 us
    ppermute x6, waiting for transfers between devices, along_z(): lax.ppermute(value, 'expert', expert_pairs(lambda y, z: (y, (z + shift) %...  99.5 us
    ppermute x6, starting transfers between devices, along_z(): lax.ppermute(value, 'expert', expert_pairs(lambda y, z: (y, (z + shift) %...  36.9 us
    ppermute x7, waiting for transfers between devices, along_y(): lax.ppermute(value, 'expert', expert_pairs(lambda y, z: ((y + shift) % Y,...  28.5 us
    ppermute x7, starting transfers between devices, along_x(): lax.ppermute(value, 'dp', dp_pairs(lambda x, c: ((x + shift) % 4, c)))  24.5 us
    pallas_call x1, Pallas kernels, body(): pl.pallas_call(merge_kernel, out_shape=shapes[n], in_specs=[whole] * 4 +...  23.8 us
    ppermute x10, starting transfers between devices, body(): pieces = near + tuple((lax.ppermute(piece, 'dp', across) for piece in near))  21.3 us
    ppermute x7, starting transfers between devices, along_y(): lax.ppermute(value, 'expert', expert_pairs(lambda y, z: ((y + shift) % Y,...  20.6 us
  transfers between devices with their start and end apart: 31, of which 9 were waited for; matrix products, arithmetic and copies ran while one was open for 3% of the time, Pallas kernels for 1%

profile of v3, /device:TPU:6, one launch (start us, length us, event | category | flops | bytes accessed | tf_op | source)
XLA Modules:
  0.0 442.4 jit_solution(18035556609571536531)
XLA Ops:
  0.6 0.8 copy.18
  1.4 0.8 copy.19
  2.1 0.2 select_reduce_fusion
  2.3 0.8 maximum_bitcast_fusion
  3.1 12.7 %collective-permute-start.2 = (bf16[1,72,256]{2,1,0:T(8,128)(2,1)S(1)}, bf16[1,72,256]{2,1,0:T(8,128)(2,1)S(1)}, u32[]{:S(2)}, u32[]{:S(2)}) collective-permute-start(bf16[1,72,256]{2,1,0:T(8,128)(2,1)S(1)} %maximum_bitcast_fusion), channel_id=1, source_target_pairs={{0,96},{8,104},{16,112},{24,120},{32,0},{40,8},{48,16},{56,24},{64... | collective-permute-start | bytes 110600 | tf_op jit(solution)/shard_map/ppermute | solution.py:255
  15.9 4.9 %collective-permute-start.1 = (bf16[1,72,256]{2,1,0:T(8,128)(2,1)S(1)}, bf16[1,72,256]{2,1,0:T(8,128)(2,1)S(1)}, u32[]{:S(2)}, u32[]{:S(2)}) collective-permute-start(bf16[1,72,256]{2,1,0:T(8,128)(2,1)S(1)} %maximum_bitcast_fusion), channel_id=1, source_target_pairs={{0,64},{8,72},{16,80},{24,88},{32,96},{40,104},{48,112},{56,120},{... | collective-permute-start | bytes 110600 | tf_op jit(solution)/shard_map/ppermute | solution.py:255
  20.8 7.8 %collective-permute-start = (bf16[1,72,256]{2,1,0:T(8,128)(2,1)S(1)}, bf16[1,72,256]{2,1,0:T(8,128)(2,1)S(1)}, u32[]{:S(2)}, u32[]{:S(2)}) collective-permute-start(bf16[1,72,256]{2,1,0:T(8,128)(2,1)S(1)} %maximum_bitcast_fusion), channel_id=1, source_target_pairs={{0,32},{8,40},{16,48},{24,56},{32,64},{40,72},{48,80},{56,88},{64,... | collective-permute-start | bytes 110600 | tf_op jit(solution)/shard_map/ppermute | solution.py:255
  28.6 0.7 and_select_fusion
  29.4 0.1 eq.51
  29.4 0.7 compare_convert_fusion.refs_3_
  30.1 0.6 fusion.refs_2_
  30.8 3.9 pack.1
  34.7 9.7 %all-to-all-start = ((bf16[64,144,128]{2,1,0:T(8,128)(2,1)}), bf16[64,144,128]{2,1,0:T(8,128)(2,1)S(1)}, u32[]{:S(2)}, u32[]{:S(2)}) async-start(bf16[64,144,128]{2,1,0:T(8,128)(2,1)} %pack.1), calls=%async_computation | async-start | bytes 4718592 | tf_op jit(solution)/shard_map/all_to_all | solution.py:282
  44.4 3.5 collective-permute-start.3
  47.9 4.3 collective-permute-start.5
  52.2 3.7 collective-permute-start.4
  55.9 96.1 %collective-permute-done.3 = bf16[4,72,256]{2,1,0:T(8,128)(2,1)S(1)} collective-permute-done((bf16[4,72,256]{2,1,0:T(8,128)(2,1)S(1)}, bf16[4,72,256]{2,1,0:T(8,128)(2,1)S(1)}, u32[]{:S(2)}, u32[]{:S(2)}) %collective-permute-start.3) | collective-permute-done | bytes 147488 | tf_op jit(solution)/shard_map/ppermute | solution.py:255
  152.0 3.4 collective-permute-done.5
  155.4 3.3 collective-permute-start.15
  158.7 1.9 collective-permute-start.14
  160.7 5.1 %collective-permute-start.13 = (bf16[16,32,256]{2,1,0:T(8,128)(2,1)S(1)}, bf16[16,32,256]{2,1,0:T(8,128)(2,1)S(1)}, u32[]{:S(2)}, u32[]{:S(2)}) collective-permute-start(bf16[16,32,256]{2,1,0:T(8,128)(2,1)S(1)} %slice.54), channel_id=1, source_target_pairs={{0,2},{1,3},{2,4},{3,5},{4,6},{5,7},{6,0},{7,1},{8,10},{9,11},{10,... | collective-permute-start | bytes 786440 | tf_op jit(solution)/shard_map/ppermute | solution.py:266
  165.8 2.2 collective-permute-done.15
  168.0 2.5 collective-permute-done.14
  170.5 1.2 pad_maximum_fusion.1.refs_9_
  171.7 4.9 %collective-permute-start.17 = (bf16[64,32,256]{2,1,0:T(8,128)(2,1)}, bf16[64,32,256]{2,1,0:T(8,128)(2,1)S(1)}, u32[]{:S(2)}, u32[]{:S(2)}) collective-permute-start(bf16[64,32,256]{2,1,0:T(8,128)(2,1)} %pad_maximum_fusion.1.refs_9_), channel_id=1, source_target_pairs={{0,384},{8,392},{16,400},{24,408},{32,416},{40,424},{48,432},{56,4... | collective-permute-start | bytes 3145736 | tf_op jit(solution)/shard_map/ppermute | solution.py:263
  176.6 1.9 collective-permute-start.16
  178.5 4.1 collective-permute-start.8
  182.7 3.0 collective-permute-start.7
  185.6 2.9 collective-permute-start.6
  188.5 23.5 %collective-permute-done.8 = bf16[16,40,256]{2,1,0:T(8,128)(2,1)S(1)} collective-permute-done((bf16[16,40,256]{2,1,0:T(8,128)(2,1)S(1)}, bf16[16,40,256]{2,1,0:T(8,128)(2,1)S(1)}, u32[]{:S(2)}, u32[]{:S(2)}) %collective-permute-start.8) | collective-permute-done | bytes 327712 | tf_op jit(solution)/shard_map/ppermute | solution.py:263
  212.0 5.0 %collective-permute-done.6 = bf16[16,40,256]{2,1,0:T(8,128)(2,1)S(1)} collective-permute-done((bf16[16,40,256]{2,1,0:T(8,128)(2,1)S(1)}, bf16[16,40,256]{2,1,0:T(8,128)(2,1)S(1)}, u32[]{:S(2)}, u32[]{:S(2)}) %collective-permute-start.6) | collective-permute-done | bytes 327712 | tf_op jit(solution)/shard_map/ppermute | solution.py:263
  217.0 0.2 pad_maximum_fusion
  217.2 1.1 slice.53.refs_4_
  218.3 2.7 collective-permute-start.10
  221.0 4.4 collective-permute-start.9
  225.4 1.9 collective-permute-start.25
  227.3 2.4 collective-permute-start.20
  229.8 0.8 slice.56
  230.6 1.9 collective-permute-start.19
  232.6 1.4 reshape.19
  234.0 1.4 copy.20
  235.4 1.1 slice.55
  236.4 7.5 %collective-permute-done.10.refs_6_ = bf16[64,32,256]{2,1,0:T(8,128)(2,1)} collective-permute-done((bf16[64,32,256]{2,1,0:T(8,128)(2,1)}, bf16[64,32,256]{2,1,0:T(8,128)(2,1)}, u32[]{:S(2)}, u32[]{:S(2)}) %collective-permute-start.10) | collective-permute-done | bytes 1048608 | tf_op jit(solution)/shard_map/ppermute | solution.py:266
  244.0 1.9 collective-permute-start.18
  245.9 1.9 collective-permute-start.27
  247.8 1.1 slice.43
  248.9 1.1 slice.44
  250.0 2.4 collective-permute-start.26
  252.4 1.9 collective-permute-start.12
  254.4 5.1 %collective-permute-start.11 = (bf16[32,32,256]{2,1,0:T(8,128)(2,1)S(1)}, bf16[32,32,256]{2,1,0:T(8,128)(2,1)}, u32[]{:S(2)}, u32[]{:S(2)}) collective-permute-start(bf16[32,32,256]{2,1,0:T(8,128)(2,1)S(1)} %slice.43), channel_id=1, source_target_pairs={{0,2},{1,3},{2,4},{3,5},{4,6},{5,7},{6,0},{7,1},{8,10},{9,11},{10,... | collective-permute-start | bytes 1572872 | tf_op jit(solution)/shard_map/ppermute | solution.py:266
  259.5 1.9 collective-permute-start.29
  261.4 8.0 %collective-permute-done.12.refs_8_ = bf16[32,32,256]{2,1,0:T(8,128)(2,1)} collective-permute-done((bf16[32,32,256]{2,1,0:T(8,128)(2,1)S(1)}, bf16[32,32,256]{2,1,0:T(8,128)(2,1)}, u32[]{:S(2)}, u32[]{:S(2)}) %collective-permute-start.12) | collective-permute-done | bytes 524320 | tf_op jit(solution)/shard_map/ppermute | solution.py:266
  269.5 1.9 collective-permute-start.21
  271.4 2.4 collective-permute-start.22
  273.8 1.0 copy-done.3
  274.8 1.9 collective-permute-start.28
  276.7 2.4 collective-permute-start.24
  279.2 2.1 collective-permute-start.23
  281.3 1.1 copy.21.refs_1_
  282.4 0.9 collective-permute-done.23.refs_17_
  283.3 1.4 copy-done
  284.7 23.8 %shard_map.103 = bf16[64,144,128]{2,1,0:T(8,128)(2,1)} custom-call(bf16[64,144,128]{2,1,0:T(8,128)(2,1)} %copy-done, f32[64,2048]{1,0:T(8,128)} %copy.21.refs_1_, bf16[16,576]{1,0:T(8,128)(2,1)} %fusion.refs_2_, bf16[64,256]{1,0:T(8,128)(2,1)} %compare_convert_fusion.refs_3_, bf16[64,32,256]{2,1,0:T(8,128)(2,1)} %slice.53.refs_4_, ...), custom_call_target="tpu_custom_call" | custom-call | tf_op jit(solution)/shard_map/pallas_call | solution.py:297
  308.5 130.0 %all_to_all.10.refs_0_ = bf16[64,144,128]{2,1,0:T(8,128)(2,1)} all-to-all(bf16[64,144,128]{2,1,0:T(8,128)(2,1)} %shard_map.103), channel_id=1, replica_groups=mesh['expert'=64,'dp'=8] {'expert'}, dimensions={0} | all-to-all | bytes 4718592 | tf_op jit(solution)/shard_map/all_to_all | solution.py:310
  438.5 3.9 unpack.1
  (40 shorter events, 0.3 us)
Async XLA Ops:
  3.1 31.5 %collective-permute-start.2 = (bf16[1,72,256]{2,1,0:T(8,128)(2,1)S(1)}, bf16[1,72,256]{2,1,0:T(8,128)(2,1)S(1)}, u32[]{:S(2)}, u32[]{:S(2)}) collective-permute-start(bf16[1,72,256]{2,1,0:T(8,128)(2,1)S(1)} %maximum_bitcast_fusion), channel_id=1, source_target_pairs={{0,96},{8,104},{16,112},{24,120},{32,0},{40,8},{48,16},{56,24},{64... | collective-permute-start | bytes 110600 | tf_op jit(solution)/shard_map/ppermute | solution.py:255
  15.9 18.8 %collective-permute-start.1 = (bf16[1,72,256]{2,1,0:T(8,128)(2,1)S(1)}, bf16[1,72,256]{2,1,0:T(8,128)(2,1)S(1)}, u32[]{:S(2)}, u32[]{:S(2)}) collective-permute-start(bf16[1,72,256]{2,1,0:T(8,128)(2,1)S(1)} %maximum_bitcast_fusion), channel_id=1, source_target_pairs={{0,64},{8,72},{16,80},{24,88},{32,96},{40,104},{48,112},{56,120},{... | collective-permute-start | bytes 110600 | tf_op jit(solution)/shard_map/ppermute | solution.py:255
  20.8 13.9 %collective-permute-start = (bf16[1,72,256]{2,1,0:T(8,128)(2,1)S(1)}, bf16[1,72,256]{2,1,0:T(8,128)(2,1)S(1)}, u32[]{:S(2)}, u32[]{:S(2)}) collective-permute-start(bf16[1,72,256]{2,1,0:T(8,128)(2,1)S(1)} %maximum_bitcast_fusion), channel_id=1, source_target_pairs={{0,32},{8,40},{16,48},{24,56},{32,64},{40,72},{48,80},{56,88},{64,... | collective-permute-start | bytes 110600 | tf_op jit(solution)/shard_map/ppermute | solution.py:255
  34.7 248.6 %all-to-all-start = ((bf16[64,144,128]{2,1,0:T(8,128)(2,1)}), bf16[64,144,128]{2,1,0:T(8,128)(2,1)S(1)}, u32[]{:S(2)}, u32[]{:S(2)}) async-start(bf16[64,144,128]{2,1,0:T(8,128)(2,1)} %pack.1), calls=%async_computation | async-start | bytes 4718592 | tf_op jit(solution)/shard_map/all_to_all | solution.py:282
  44.4 107.5 %collective-permute-start.3 = (bf16[4,72,256]{2,1,0:T(8,128)(2,1)S(1)}, bf16[4,72,256]{2,1,0:T(8,128)(2,1)S(1)}, u32[]{:S(2)}, u32[]{:S(2)}) collective-permute-start(bf16[4,72,256]{2,1,0:T(8,128)(2,1)S(1)} %pad_maximum_fusion.2), channel_id=1, source_target_pairs={{0,8},{8,16},{16,24},{24,32},{32,40},{40,48},{48,56},{56,64},{64,7... | collective-permute-start | bytes 442376 | tf_op jit(solution)/shard_map/ppermute | solution.py:255
  47.9 107.5 %collective-permute-start.5 = (bf16[4,72,256]{2,1,0:T(8,128)(2,1)S(1)}, bf16[4,72,256]{2,1,0:T(8,128)(2,1)S(1)}, u32[]{:S(2)}, u32[]{:S(2)}) collective-permute-start(bf16[4,72,256]{2,1,0:T(8,128)(2,1)S(1)} %pad_maximum_fusion.2), channel_id=1, source_target_pairs={{0,16},{8,24},{16,32},{24,40},{32,48},{40,56},{48,64},{56,72},{64,... | collective-permute-start | bytes 442376 | tf_op jit(solution)/shard_map/ppermute | solution.py:255
  52.2 99.8 %collective-permute-start.4 = (bf16[4,72,256]{2,1,0:T(8,128)(2,1)S(1)}, bf16[4,72,256]{2,1,0:T(8,128)(2,1)S(1)}, u32[]{:S(2)}, u32[]{:S(2)}) collective-permute-start(bf16[4,72,256]{2,1,0:T(8,128)(2,1)S(1)} %pad_maximum_fusion.2), channel_id=1, source_target_pairs={{0,120},{8,0},{16,8},{24,16},{32,24},{40,32},{48,40},{56,48},{64,5... | collective-permute-start | bytes 442376 | tf_op jit(solution)/shard_map/ppermute | solution.py:255
  155.4 12.6 %collective-permute-start.15 = (bf16[16,32,256]{2,1,0:T(8,128)(2,1)S(1)}, bf16[16,32,256]{2,1,0:T(8,128)(2,1)S(1)}, u32[]{:S(2)}, u32[]{:S(2)}) collective-permute-start(bf16[16,32,256]{2,1,0:T(8,128)(2,1)S(1)} %slice.54), channel_id=1, source_target_pairs={{0,4},{1,5},{2,6},{3,7},{4,0},{5,1},{6,2},{7,3},{8,12},{9,13},{10,... | collective-permute-start | bytes 786440 | tf_op jit(solution)/shard_map/ppermute | solution.py:266
  158.7 11.8 %collective-permute-start.14 = (bf16[16,32,256]{2,1,0:T(8,128)(2,1)S(1)}, bf16[16,32,256]{2,1,0:T(8,128)(2,1)S(1)}, u32[]{:S(2)}, u32[]{:S(2)}) collective-permute-start(bf16[16,32,256]{2,1,0:T(8,128)(2,1)S(1)} %slice.54), channel_id=1, source_target_pairs={{0,6},{1,7},{2,0},{3,1},{4,2},{5,3},{6,4},{7,5},{8,14},{9,15},{10,... | collective-permute-start | bytes 786440 | tf_op jit(solution)/shard_map/ppermute | solution.py:266
  160.7 9.8 %collective-permute-start.13 = (bf16[16,32,256]{2,1,0:T(8,128)(2,1)S(1)}, bf16[16,32,256]{2,1,0:T(8,128)(2,1)S(1)}, u32[]{:S(2)}, u32[]{:S(2)}) collective-permute-start(bf16[16,32,256]{2,1,0:T(8,128)(2,1)S(1)} %slice.54), channel_id=1, source_target_pairs={{0,2},{1,3},{2,4},{3,5},{4,6},{5,7},{6,0},{7,1},{8,10},{9,11},{10,... | collective-permute-start | bytes 786440 | tf_op jit(solution)/shard_map/ppermute | solution.py:266
  171.7 55.6 %collective-permute-start.17 = (bf16[64,32,256]{2,1,0:T(8,128)(2,1)}, bf16[64,32,256]{2,1,0:T(8,128)(2,1)S(1)}, u32[]{:S(2)}, u32[]{:S(2)}) collective-permute-start(bf16[64,32,256]{2,1,0:T(8,128)(2,1)} %pad_maximum_fusion.1.refs_9_), channel_id=1, source_target_pairs={{0,384},{8,392},{16,400},{24,408},{32,416},{40,424},{48,432},{56,4... | collective-permute-start | bytes 3145736 | tf_op jit(solution)/shard_map/ppermute | solution.py:263
  176.6 54.0 %collective-permute-start.16 = (bf16[64,32,256]{2,1,0:T(8,128)(2,1)}, bf16[64,32,256]{2,1,0:T(8,128)(2,1)}, u32[]{:S(2)}, u32[]{:S(2)}) collective-permute-start(bf16[64,32,256]{2,1,0:T(8,128)(2,1)} %pad_maximum_fusion.1.refs_9_), channel_id=1, source_target_pairs={{0,128},{8,136},{16,144},{24,152},{32,160},{40,168},{48,176},{56,1... | collective-permute-start | bytes 3145736 | tf_op jit(solution)/shard_map/ppermute | solution.py:263
  178.5 33.4 %collective-permute-start.8 = (bf16[16,40,256]{2,1,0:T(8,128)(2,1)S(1)}, bf16[16,40,256]{2,1,0:T(8,128)(2,1)S(1)}, u32[]{:S(2)}, u32[]{:S(2)}) collective-permute-start(bf16[16,40,256]{2,1,0:T(8,128)(2,1)S(1)} %slice.52), channel_id=1, source_target_pairs={{0,256},{8,264},{16,272},{24,280},{32,288},{40,296},{48,304},{56,3... | collective-permute-start | bytes 983048 | tf_op jit(solution)/shard_map/ppermute | solution.py:263
  182.7 29.3 %collective-permute-start.7 = (bf16[16,40,256]{2,1,0:T(8,128)(2,1)S(1)}, bf16[16,40,256]{2,1,0:T(8,128)(2,1)S(1)}, u32[]{:S(2)}, u32[]{:S(2)}) collective-permute-start(bf16[16,40,256]{2,1,0:T(8,128)(2,1)S(1)} %slice.52), channel_id=1, source_target_pairs={{0,384},{8,392},{16,400},{24,408},{32,416},{40,424},{48,432},{56,4... | collective-permute-start | bytes 983048 | tf_op jit(solution)/shard_map/ppermute | solution.py:263
  185.6 31.4 %collective-permute-start.6 = (bf16[16,40,256]{2,1,0:T(8,128)(2,1)S(1)}, bf16[16,40,256]{2,1,0:T(8,128)(2,1)S(1)}, u32[]{:S(2)}, u32[]{:S(2)}) collective-permute-start(bf16[16,40,256]{2,1,0:T(8,128)(2,1)S(1)} %slice.52), channel_id=1, source_target_pairs={{0,128},{8,136},{16,144},{24,152},{32,160},{40,168},{48,176},{56,1... | collective-permute-start | bytes 983048 | tf_op jit(solution)/shard_map/ppermute | solution.py:263
  218.3 25.6 %collective-permute-start.10 = (bf16[64,32,256]{2,1,0:T(8,128)(2,1)}, bf16[64,32,256]{2,1,0:T(8,128)(2,1)}, u32[]{:S(2)}, u32[]{:S(2)}) collective-permute-start(bf16[64,32,256]{2,1,0:T(8,128)(2,1)} %slice.53.refs_4_), channel_id=1, source_target_pairs={{0,6},{1,7},{2,0},{3,1},{4,2},{5,3},{6,4},{7,5},{8,14},{9,15},{10,... | collective-permute-start | bytes 3145736 | tf_op jit(solution)/shard_map/ppermute | solution.py:266
  221.0 24.9 %collective-permute-start.9 = (bf16[64,32,256]{2,1,0:T(8,128)(2,1)}, bf16[64,32,256]{2,1,0:T(8,128)(2,1)}, u32[]{:S(2)}, u32[]{:S(2)}) collective-permute-start(bf16[64,32,256]{2,1,0:T(8,128)(2,1)} %slice.53.refs_4_), channel_id=1, source_target_pairs={{0,2},{1,3},{2,4},{3,5},{4,6},{5,7},{6,0},{7,1},{8,10},{9,11},{10,... | collective-permute-start | bytes 3145736 | tf_op jit(solution)/shard_map/ppermute | solution.py:266
  225.4 24.6 %collective-permute-start.25 = (bf16[64,32,256]{2,1,0:T(8,128)(2,1)}, bf16[64,32,256]{2,1,0:T(8,128)(2,1)}, u32[]{:S(2)}, u32[]{:S(2)}) collective-permute-start(bf16[64,32,256]{2,1,0:T(8,128)(2,1)} %pad_maximum_fusion.1.refs_9_), channel_id=1, source_target_pairs={{0,1},{1,0},{2,3},{3,2},{4,5},{5,4},{6,7},{7,6},{8,9},{9,8},{10,11... | collective-permute-start | bytes 3145736 | tf_op jit(solution)/shard_map/ppermute | solution.py:291
  227.3 2.4 copy-start.1
  227.3 25.1 %collective-permute-start.20 = (bf16[64,32,256]{2,1,0:T(8,128)(2,1)}, bf16[64,32,256]{2,1,0:T(8,128)(2,1)}, u32[]{:S(2)}, u32[]{:S(2)}) collective-permute-start(bf16[64,32,256]{2,1,0:T(8,128)(2,1)} %slice.53.refs_4_), channel_id=1, source_target_pairs={{0,1},{1,0},{2,3},{3,2},{4,5},{5,4},{6,7},{7,6},{8,9},{9,8},{10,11... | collective-permute-start | bytes 3145736 | tf_op jit(solution)/shard_map/ppermute | solution.py:291
  230.6 23.8 %collective-permute-start.19 = (bf16[32,32,256]{2,1,0:T(8,128)(2,1)}, bf16[32,32,256]{2,1,0:T(8,128)(2,1)}, u32[]{:S(2)}, u32[]{:S(2)}) collective-permute-start(bf16[32,32,256]{2,1,0:T(8,128)(2,1)} %slice.56), channel_id=1, source_target_pairs={{0,384},{8,392},{16,400},{24,408},{32,416},{40,424},{48,432},{56,4... | collective-permute-start | bytes 1572872 | tf_op jit(solution)/shard_map/ppermute | solution.py:263
  234.0 11.9 %copy-start.2 = (bf16[64,32,256]{2,1,0:T(8,128)(2,1)S(1)}, bf16[64,32,256]{2,1,0:T(8,128)(2,1)}, u32[]{:S(2)}) copy-start(bf16[64,32,256]{2,1,0:T(8,128)(2,1)} %copy-done.1) | copy-start | bytes 3145732
  244.0 15.5 %collective-permute-start.18 = (bf16[32,32,256]{2,1,0:T(8,128)(2,1)S(1)}, bf16[32,32,256]{2,1,0:T(8,128)(2,1)}, u32[]{:S(2)}, u32[]{:S(2)}) collective-permute-start(bf16[32,32,256]{2,1,0:T(8,128)(2,1)S(1)} %slice.55), channel_id=1, source_target_pairs={{0,128},{8,136},{16,144},{24,152},{32,160},{40,168},{48,176},{56,1... | collective-permute-start | bytes 1572872 | tf_op jit(solution)/shard_map/ppermute | solution.py:263
  245.9 27.9 %collective-permute-start.27 = (bf16[64,32,256]{2,1,0:T(8,128)(2,1)S(1)}, bf16[64,32,256]{2,1,0:T(8,128)(2,1)S(1)}, u32[]{:S(2)}, u32[]{:S(2)}) collective-permute-start(bf16[64,32,256]{2,1,0:T(8,128)(2,1)S(1)} %copy-done.2), channel_id=1, source_target_pairs={{0,1},{1,0},{2,3},{3,2},{4,5},{5,4},{6,7},{7,6},{8,9},{9,8},{10,11... | collective-permute-start | bytes 3145736 | tf_op jit(solution)/shard_map/ppermute | solution.py:291
  250.0 26.7 %collective-permute-start.26 = (bf16[64,32,256]{2,1,0:T(8,128)(2,1)}, bf16[64,32,256]{2,1,0:T(8,128)(2,1)}, u32[]{:S(2)}, u32[]{:S(2)}) collective-permute-start(bf16[64,32,256]{2,1,0:T(8,128)(2,1)} %collective-permute-done.16.refs_10_), channel_id=1, source_target_pairs={{0,1},{1,0},{2,3},{3,2},{4,5},{5,4},{6,7},{7,6},{8,9},{9,8},{10,11... | collective-permute-start | bytes 3145736 | tf_op jit(solution)/shard_map/ppermute | solution.py:291
  252.4 17.1 %collective-permute-start.12 = (bf16[32,32,256]{2,1,0:T(8,128)(2,1)S(1)}, bf16[32,32,256]{2,1,0:T(8,128)(2,1)}, u32[]{:S(2)}, u32[]{:S(2)}) collective-permute-start(bf16[32,32,256]{2,1,0:T(8,128)(2,1)S(1)} %slice.44), channel_id=1, source_target_pairs={{0,6},{1,7},{2,0},{3,1},{4,2},{5,3},{6,4},{7,5},{8,14},{9,15},{10,... | collective-permute-start | bytes 1572872 | tf_op jit(solution)/shard_map/ppermute | solution.py:266
  254.4 17.0 %collective-permute-start.11 = (bf16[32,32,256]{2,1,0:T(8,128)(2,1)S(1)}, bf16[32,32,256]{2,1,0:T(8,128)(2,1)}, u32[]{:S(2)}, u32[]{:S(2)}) collective-permute-start(bf16[32,32,256]{2,1,0:T(8,128)(2,1)S(1)} %slice.43), channel_id=1, source_target_pairs={{0,2},{1,3},{2,4},{3,5},{4,6},{5,7},{6,0},{7,1},{8,10},{9,11},{10,... | collective-permute-start | bytes 1572872 | tf_op jit(solution)/shard_map/ppermute | solution.py:266
  259.5 19.6 %collective-permute-start.29 = (bf16[32,32,256]{2,1,0:T(8,128)(2,1)}, bf16[32,32,256]{2,1,0:T(8,128)(2,1)}, u32[]{:S(2)}, u32[]{:S(2)}) collective-permute-start(bf16[32,32,256]{2,1,0:T(8,128)(2,1)} %collective-permute-done.19.refs_13_), channel_id=1, source_target_pairs={{0,1},{1,0},{2,3},{3,2},{4,5},{5,4},{6,7},{7,6},{8,9},{9,8},{10,11... | collective-permute-start | bytes 1572872 | tf_op jit(solution)/shard_map/ppermute | solution.py:291
  269.5 13.8 %collective-permute-start.21 = (bf16[64,32,256]{2,1,0:T(8,128)(2,1)}, bf16[64,32,256]{2,1,0:T(8,128)(2,1)}, u32[]{:S(2)}, u32[]{:S(2)}) collective-permute-start(bf16[64,32,256]{2,1,0:T(8,128)(2,1)} %collective-permute-done.9.refs_5_), channel_id=1, source_target_pairs={{0,1},{1,0},{2,3},{3,2},{4,5},{5,4},{6,7},{7,6},{8,9},{9,8},{10,11... | collective-permute-start | bytes 3145736 | tf_op jit(solution)/shard_map/ppermute | solution.py:291
  271.4 11.9 %collective-permute-start.22 = (bf16[64,32,256]{2,1,0:T(8,128)(2,1)}, bf16[64,32,256]{2,1,0:T(8,128)(2,1)}, u32[]{:S(2)}, u32[]{:S(2)}) collective-permute-start(bf16[64,32,256]{2,1,0:T(8,128)(2,1)} %collective-permute-done.10.refs_6_), channel_id=1, source_target_pairs={{0,1},{1,0},{2,3},{3,2},{4,5},{5,4},{6,7},{7,6},{8,9},{9,8},{10,11... | collective-permute-start | bytes 3145736 | tf_op jit(solution)/shard_map/ppermute | solution.py:291
  273.8 1.0 copy-start.3
  274.8 7.6 %collective-permute-start.28 = (bf16[32,32,256]{2,1,0:T(8,128)(2,1)}, bf16[32,32,256]{2,1,0:T(8,128)(2,1)}, u32[]{:S(2)}, u32[]{:S(2)}) collective-permute-start(bf16[32,32,256]{2,1,0:T(8,128)(2,1)} %collective-permute-done.18.refs_12_), channel_id=1, source_target_pairs={{0,1},{1,0},{2,3},{3,2},{4,5},{5,4},{6,7},{7,6},{8,9},{9,8},{10,11... | collective-permute-start | bytes 1572872 | tf_op jit(solution)/shard_map/ppermute | solution.py:291
  276.7 5.7 %collective-permute-start.24 = (bf16[32,32,256]{2,1,0:T(8,128)(2,1)}, bf16[32,32,256]{2,1,0:T(8,128)(2,1)}, u32[]{:S(2)}, u32[]{:S(2)}) collective-permute-start(bf16[32,32,256]{2,1,0:T(8,128)(2,1)} %collective-permute-done.12.refs_8_), channel_id=1, source_target_pairs={{0,1},{1,0},{2,3},{3,2},{4,5},{5,4},{6,7},{7,6},{8,9},{9,8},{10,11... | collective-permute-start | bytes 1572872 | tf_op jit(solution)/shard_map/ppermute | solution.py:291
  279.2 4.1 collective-permute-start.23
  283.3 1.4 copy-start

commit v4 on v3

--- a/solution.py
+++ b/solution.py
@@ -245,19 +245,18 @@
     belongs_col = (cluster[:, None] == jnp.tile(clusters, TILES)[None, :]).astype(jnp.bfloat16)
     belongs_row = (clusters[:, None] == jnp.tile(cluster, 3 * ROWS)[None, :]).astype(jnp.bfloat16)
 
-    chosen = routes[:, :, None] == jnp.arange(EXPERTS, dtype=jnp.int32)[None, None, :]
-    share = jnp.sum(jnp.where(chosen, route_weights.astype(jnp.float32)[:, :, None], 0.0), axis=1)
+    ids = jnp.arange(EXPERTS, dtype=jnp.int32)[None, :, None]
+    weight = route_weights.T.astype(jnp.float32)[:, None, :]
+    share = jnp.sum(jnp.where(routes.T[:, None, :] == ids, weight, 0.0), axis=0)
     share = share.astype(jnp.bfloat16)
-    share = jnp.concatenate([share[8 * i : 8 * i + 8] for i in range(4)], axis=1)
+    share = jnp.concatenate([share[8 * i : 8 * i + 8] for i in range(8)], axis=1)
     block = jnp.concatenate([tokens, share, cotangent], axis=0)[None]
 
     def along_z(value, shift):
         return lax.ppermute(value, "expert", expert_pairs(lambda y, z: (y, (z + shift) % Z)))
 
     block = jnp.concatenate([block] + [along_z(block, shift) for shift in (4, 8, 12)], axis=0)
-    packed, block, belongs_row, belongs_col = lax.optimization_barrier(
-        (packed, block, belongs_row, belongs_col)
-    )
+    packed, block = lax.optimization_barrier((packed, block))
 
     def along_y(value, shift):
         return lax.ppermute(value, "expert", expert_pairs(lambda y, z: ((y + shift) % Y, z)))
@@ -282,10 +281,12 @@
         received.append(lax.all_to_all(part, "expert", split_axis=0, concat_axis=0, tiled=True))
     tok_block = whole_ring(block[:, : BLOCK + 8], along_y)
     cot_block = whole_ring(block[:, BLOCK + 8 :], along_x)
-    share = tok_block[:, BLOCK:].reshape(EXPERTS, 8, 4, EXPERTS).transpose(3, 0, 2, 1)
+    share = tok_block[:, BLOCK:].reshape(EXPERTS, 8, 8, BLOCK).transpose(2, 1, 0, 3)
     share = share.reshape(EXPERTS, EXPERTS * BLOCK).astype(jnp.float32)
     cot_near, _ = split_ring(cot_block, along_y)
-    tok_near, share = split_ring(tok_block[:, :BLOCK], along_x, share)
+    tables = (share, belongs_row, belongs_col)
+    tok_near, tables = split_ring(tok_block[:, :BLOCK], along_x, tables)
+    share, belongs_row, belongs_col = tables
     near = tok_near + cot_near
     across = dp_pairs(lambda x, c: (x, 1 - c))
     pieces = near + tuple(lax.ppermute(piece, "dp", across) for piece in near)

time: 446 us -> 446 us (level)
  waiting for transfers between devices: 149 us -> 140 us
    ppermute x7, waiting for transfers between devices: 20.3 us -> 12 us  [along_x(): lax.ppermute(value, 'dp', dp_pairs(lambda x, c: ((x + shift) % 4, c)))]
  transfers between devices with their start and end apart: 31 -> 31, of which waited for: 9 -> 8; matrix products, arithmetic and copies ran while one was open for 3% -> 4% of each run, Pallas kernels for 1% -> 1%
where the time goes in v4:
time: 446 us; the launch traced here: 442 us
  waiting for transfers between devices  140 us (31%)
  blocking collectives  129 us (29%)
  starting transfers between devices  117 us (26%)
  Pallas kernels  31.5 us (7%)
  local copies, waits for them, and re-layouts  17 us (4%)
  other arithmetic  5.76 us (1%)
    all_to_all x1, blocking collectives, body(): lax.all_to_all(answer, 'expert', split_axis=0, concat_axis=0, tiled=True)  129 us
    ppermute x6, waiting for transfers between devices, along_z(): lax.ppermute(value, 'expert', expert_pairs(lambda y, z: (y, (z + shift) %...  98.8 us
    ppermute x6, starting transfers between devices, along_z(): lax.ppermute(value, 'expert', expert_pairs(lambda y, z: (y, (z + shift) %...  36.9 us
    ppermute x7, waiting for transfers between devices, along_y(): lax.ppermute(value, 'expert', expert_pairs(lambda y, z: ((y + shift) % Y,...  27.9 us
    ppermute x7, starting transfers between devices, along_x(): lax.ppermute(value, 'dp', dp_pairs(lambda x, c: ((x + shift) % 4, c)))  24.5 us
    pallas_call x1, Pallas kernels, body(): pl.pallas_call(merge_kernel, out_shape=shapes[n], in_specs=[whole] * 4 +...  23.8 us
    ppermute x7, starting transfers between devices, along_y(): lax.ppermute(value, 'expert', expert_pairs(lambda y, z: ((y + shift) % Y,...  22.6 us
    ppermute x10, starting transfers between devices, body(): pieces = near + tuple((lax.ppermute(piece, 'dp', across) for piece in near))  21.3 us
  transfers between devices with their start and end apart: 31, of which 8 were waited for; matrix products, arithmetic and copies ran while one was open for 4% of the time, Pallas kernels for 1%

profile of v4, /device:TPU:6, one launch (start us, length us, event | category | flops | bytes accessed | tf_op | source)
XLA Modules:
  0.0 441.7 jit_solution(1130942141421192976)
XLA Ops:
  0.6 0.7 convert_bitcast_fusion
  1.3 0.8 select_reduce_fusion
  2.1 0.1 copy.14
  2.3 0.7 maximum_bitcast_fusion
  3.1 12.7 %collective-permute-start.2 = (bf16[1,72,256]{2,1,0:T(8,128)(2,1)S(1)}, bf16[1,72,256]{2,1,0:T(8,128)(2,1)S(1)}, u32[]{:S(2)}, u32[]{:S(2)}) collective-permute-start(bf16[1,72,256]{2,1,0:T(8,128)(2,1)S(1)} %maximum_bitcast_fusion), channel_id=1, source_target_pairs={{0,96},{8,104},{16,112},{24,120},{32,0},{40,8},{48,16},{56,24},{64... | collective-permute-start | bytes 110600 | tf_op jit(solution)/shard_map/ppermute | solution.py:256
  15.8 4.9 %collective-permute-start.1 = (bf16[1,72,256]{2,1,0:T(8,128)(2,1)S(1)}, bf16[1,72,256]{2,1,0:T(8,128)(2,1)S(1)}, u32[]{:S(2)}, u32[]{:S(2)}) collective-permute-start(bf16[1,72,256]{2,1,0:T(8,128)(2,1)S(1)} %maximum_bitcast_fusion), channel_id=1, source_target_pairs={{0,64},{8,72},{16,80},{24,88},{32,96},{40,104},{48,112},{56,120},{... | collective-permute-start | bytes 110600 | tf_op jit(solution)/shard_map/ppermute | solution.py:256
  20.7 7.8 %collective-permute-start = (bf16[1,72,256]{2,1,0:T(8,128)(2,1)S(1)}, bf16[1,72,256]{2,1,0:T(8,128)(2,1)S(1)}, u32[]{:S(2)}, u32[]{:S(2)}) collective-permute-start(bf16[1,72,256]{2,1,0:T(8,128)(2,1)S(1)} %maximum_bitcast_fusion), channel_id=1, source_target_pairs={{0,32},{8,40},{16,48},{24,56},{32,64},{40,72},{48,80},{56,88},{64,... | collective-permute-start | bytes 110600 | tf_op jit(solution)/shard_map/ppermute | solution.py:256
  28.6 3.9 pack.1
  32.5 11.8 %all-to-all-start = ((bf16[64,144,128]{2,1,0:T(8,128)(2,1)}), bf16[64,144,128]{2,1,0:T(8,128)(2,1)S(1)}, u32[]{:S(2)}, u32[]{:S(2)}) async-start(bf16[64,144,128]{2,1,0:T(8,128)(2,1)} %pack.1), calls=%async_computation | async-start | bytes 4718592 | tf_op jit(solution)/shard_map/all_to_all | solution.py:281
  44.3 3.5 collective-permute-start.3
  47.8 4.3 collective-permute-start.5
  52.1 3.7 collective-permute-start.4
  55.8 95.3 %collective-permute-done.3 = bf16[4,72,256]{2,1,0:T(8,128)(2,1)S(1)} collective-permute-done((bf16[4,72,256]{2,1,0:T(8,128)(2,1)S(1)}, bf16[4,72,256]{2,1,0:T(8,128)(2,1)S(1)}, u32[]{:S(2)}, u32[]{:S(2)}) %collective-permute-start.3) | collective-permute-done | bytes 147488 | tf_op jit(solution)/shard_map/ppermute | solution.py:256
  151.2 3.4 collective-permute-done.5
  154.7 3.3 collective-permute-start.15
  158.0 1.9 collective-permute-start.14
  159.9 5.1 %collective-permute-start.13 = (bf16[16,32,256]{2,1,0:T(8,128)(2,1)S(1)}, bf16[16,32,256]{2,1,0:T(8,128)(2,1)S(1)}, u32[]{:S(2)}, u32[]{:S(2)}) collective-permute-start(bf16[16,32,256]{2,1,0:T(8,128)(2,1)S(1)} %slice.74), channel_id=1, source_target_pairs={{0,2},{1,3},{2,4},{3,5},{4,6},{5,7},{6,0},{7,1},{8,10},{9,11},{10,... | collective-permute-start | bytes 786440 | tf_op jit(solution)/shard_map/ppermute | solution.py:265
  165.1 1.5 collective-permute-done.15
  166.6 2.5 collective-permute-done.14
  169.2 1.2 pad_maximum_fusion.1.refs_9_
  170.4 4.8 %collective-permute-start.17 = (bf16[64,32,256]{2,1,0:T(8,128)(2,1)}, bf16[64,32,256]{2,1,0:T(8,128)(2,1)}, u32[]{:S(2)}, u32[]{:S(2)}) collective-permute-start(bf16[64,32,256]{2,1,0:T(8,128)(2,1)} %pad_maximum_fusion.1.refs_9_), channel_id=1, source_target_pairs={{0,384},{8,392},{16,400},{24,408},{32,416},{40,424},{48,432},{56,4... | collective-permute-start | bytes 3145736 | tf_op jit(solution)/shard_map/ppermute | solution.py:262
  175.2 1.9 collective-permute-start.16
  177.2 4.1 collective-permute-start.8
  181.3 3.0 collective-permute-start.7
  184.3 2.9 collective-permute-start.6
  187.2 23.4 %collective-permute-done.8 = bf16[16,40,256]{2,1,0:T(8,128)(2,1)S(1)} collective-permute-done((bf16[16,40,256]{2,1,0:T(8,128)(2,1)S(1)}, bf16[16,40,256]{2,1,0:T(8,128)(2,1)S(1)}, u32[]{:S(2)}, u32[]{:S(2)}) %collective-permute-start.8) | collective-permute-done | bytes 327712 | tf_op jit(solution)/shard_map/ppermute | solution.py:262
  210.6 4.4 %collective-permute-done.6 = bf16[16,40,256]{2,1,0:T(8,128)(2,1)S(1)} collective-permute-done((bf16[16,40,256]{2,1,0:T(8,128)(2,1)S(1)}, bf16[16,40,256]{2,1,0:T(8,128)(2,1)S(1)}, u32[]{:S(2)}, u32[]{:S(2)}) %collective-permute-start.6) | collective-permute-done | bytes 327712 | tf_op jit(solution)/shard_map/ppermute | solution.py:262
  215.0 0.2 pad_maximum_fusion
  215.2 0.6 copy-done.1
  215.8 1.1 slice.73.refs_4_
  216.9 3.9 collective-permute-start.10
  220.8 3.1 collective-permute-start.9
  224.0 1.9 collective-permute-start.25
  225.9 2.4 collective-permute-start.20
  228.5 1.9 slice.76
  230.4 1.9 collective-permute-start.19
  232.4 0.6 fusion.refs_2_
  233.0 0.7 compare_convert_fusion.refs_3_
  233.6 0.8 maximum_convert_fusion
  234.5 1.4 copy.15
  235.9 2.0 copy.16
  237.9 3.1 reshape.18.refs_1_
  241.0 1.1 slice.75
  242.1 3.9 collective-permute-start.18
  246.0 1.9 collective-permute-start.27
  247.9 1.1 slice.59
  249.0 1.1 slice.60
  250.1 2.4 collective-permute-start.26
  252.5 2.7 collective-permute-start.12
  255.3 4.3 collective-permute-start.11
  259.6 1.9 collective-permute-start.29
  261.6 7.9 %collective-permute-done.12.refs_8_ = bf16[32,32,256]{2,1,0:T(8,128)(2,1)S(1)} collective-permute-done((bf16[32,32,256]{2,1,0:T(8,128)(2,1)S(1)}, bf16[32,32,256]{2,1,0:T(8,128)(2,1)S(1)}, u32[]{:S(2)}, u32[]{:S(2)}) %collective-permute-start.12) | collective-permute-done | bytes 524320 | tf_op jit(solution)/shard_map/ppermute | solution.py:265
  269.5 1.9 collective-permute-start.21
  271.4 2.4 collective-permute-start.22
  273.9 1.9 collective-permute-start.28
  275.8 2.4 collective-permute-start.24
  278.2 2.1 collective-permute-start.23
  280.4 1.7 collective-permute-done.23.refs_17_
  282.1 0.7 copy-done.12
  282.9 1.0 copy-done.5
  283.9 1.4 copy-done
  285.3 23.8 %shard_map.103 = bf16[64,144,128]{2,1,0:T(8,128)(2,1)} custom-call(bf16[64,144,128]{2,1,0:T(8,128)(2,1)} %copy-done, f32[64,2048]{1,0:T(8,128)} %reshape.18.refs_1_, bf16[16,576]{1,0:T(8,128)(2,1)} %fusion.refs_2_, bf16[64,256]{1,0:T(8,128)(2,1)} %compare_convert_fusion.refs_3_, bf16[64,32,256]{2,1,0:T(8,128)(2,1)} %slice.73.refs_4_, ...), custom_call_target="tpu_custom_call" | custom-call | tf_op jit(solution)/shard_map/pallas_call | solution.py:298
  309.0 128.8 %all_to_all.10.refs_0_ = bf16[64,144,128]{2,1,0:T(8,128)(2,1)} all-to-all(bf16[64,144,128]{2,1,0:T(8,128)(2,1)} %shard_map.103), channel_id=1, replica_groups=mesh['expert'=64,'dp'=8] {'expert'}, dimensions={0} | all-to-all | bytes 4718592 | tf_op jit(solution)/shard_map/all_to_all | solution.py:311
  437.9 3.9 unpack.1
  (61 shorter events, 0.5 us)
Async XLA Ops:
  3.1 29.4 %collective-permute-start.2 = (bf16[1,72,256]{2,1,0:T(8,128)(2,1)S(1)}, bf16[1,72,256]{2,1,0:T(8,128)(2,1)S(1)}, u32[]{:S(2)}, u32[]{:S(2)}) collective-permute-start(bf16[1,72,256]{2,1,0:T(8,128)(2,1)S(1)} %maximum_bitcast_fusion), channel_id=1, source_target_pairs={{0,96},{8,104},{16,112},{24,120},{32,0},{40,8},{48,16},{56,24},{64... | collective-permute-start | bytes 110600 | tf_op jit(solution)/shard_map/ppermute | solution.py:256
  15.8 16.7 %collective-permute-start.1 = (bf16[1,72,256]{2,1,0:T(8,128)(2,1)S(1)}, bf16[1,72,256]{2,1,0:T(8,128)(2,1)S(1)}, u32[]{:S(2)}, u32[]{:S(2)}) collective-permute-start(bf16[1,72,256]{2,1,0:T(8,128)(2,1)S(1)} %maximum_bitcast_fusion), channel_id=1, source_target_pairs={{0,64},{8,72},{16,80},{24,88},{32,96},{40,104},{48,112},{56,120},{... | collective-permute-start | bytes 110600 | tf_op jit(solution)/shard_map/ppermute | solution.py:256
  20.7 11.8 %collective-permute-start = (bf16[1,72,256]{2,1,0:T(8,128)(2,1)S(1)}, bf16[1,72,256]{2,1,0:T(8,128)(2,1)S(1)}, u32[]{:S(2)}, u32[]{:S(2)}) collective-permute-start(bf16[1,72,256]{2,1,0:T(8,128)(2,1)S(1)} %maximum_bitcast_fusion), channel_id=1, source_target_pairs={{0,32},{8,40},{16,48},{24,56},{32,64},{40,72},{48,80},{56,88},{64,... | collective-permute-start | bytes 110600 | tf_op jit(solution)/shard_map/ppermute | solution.py:256
  32.5 251.3 %all-to-all-start = ((bf16[64,144,128]{2,1,0:T(8,128)(2,1)}), bf16[64,144,128]{2,1,0:T(8,128)(2,1)S(1)}, u32[]{:S(2)}, u32[]{:S(2)}) async-start(bf16[64,144,128]{2,1,0:T(8,128)(2,1)} %pack.1), calls=%async_computation | async-start | bytes 4718592 | tf_op jit(solution)/shard_map/all_to_all | solution.py:281
  44.3 106.8 %collective-permute-start.3 = (bf16[4,72,256]{2,1,0:T(8,128)(2,1)S(1)}, bf16[4,72,256]{2,1,0:T(8,128)(2,1)S(1)}, u32[]{:S(2)}, u32[]{:S(2)}) collective-permute-start(bf16[4,72,256]{2,1,0:T(8,128)(2,1)S(1)} %pad_maximum_fusion.2), channel_id=1, source_target_pairs={{0,8},{8,16},{16,24},{24,32},{32,40},{40,48},{48,56},{56,64},{64,7... | collective-permute-start | bytes 442376 | tf_op jit(solution)/shard_map/ppermute | solution.py:256
  47.8 106.8 %collective-permute-start.5 = (bf16[4,72,256]{2,1,0:T(8,128)(2,1)S(1)}, bf16[4,72,256]{2,1,0:T(8,128)(2,1)S(1)}, u32[]{:S(2)}, u32[]{:S(2)}) collective-permute-start(bf16[4,72,256]{2,1,0:T(8,128)(2,1)S(1)} %pad_maximum_fusion.2), channel_id=1, source_target_pairs={{0,16},{8,24},{16,32},{24,40},{32,48},{40,56},{48,64},{56,72},{64,... | collective-permute-start | bytes 442376 | tf_op jit(solution)/shard_map/ppermute | solution.py:256
  52.1 99.1 %collective-permute-start.4 = (bf16[4,72,256]{2,1,0:T(8,128)(2,1)S(1)}, bf16[4,72,256]{2,1,0:T(8,128)(2,1)S(1)}, u32[]{:S(2)}, u32[]{:S(2)}) collective-permute-start(bf16[4,72,256]{2,1,0:T(8,128)(2,1)S(1)} %pad_maximum_fusion.2), channel_id=1, source_target_pairs={{0,120},{8,0},{16,8},{24,16},{32,24},{40,32},{48,40},{56,48},{64,5... | collective-permute-start | bytes 442376 | tf_op jit(solution)/shard_map/ppermute | solution.py:256
  154.7 11.9 %collective-permute-start.15 = (bf16[16,32,256]{2,1,0:T(8,128)(2,1)S(1)}, bf16[16,32,256]{2,1,0:T(8,128)(2,1)S(1)}, u32[]{:S(2)}, u32[]{:S(2)}) collective-permute-start(bf16[16,32,256]{2,1,0:T(8,128)(2,1)S(1)} %slice.74), channel_id=1, source_target_pairs={{0,4},{1,5},{2,6},{3,7},{4,0},{5,1},{6,2},{7,3},{8,12},{9,13},{10,... | collective-permute-start | bytes 786440 | tf_op jit(solution)/shard_map/ppermute | solution.py:265
  158.0 11.2 %collective-permute-start.14 = (bf16[16,32,256]{2,1,0:T(8,128)(2,1)S(1)}, bf16[16,32,256]{2,1,0:T(8,128)(2,1)S(1)}, u32[]{:S(2)}, u32[]{:S(2)}) collective-permute-start(bf16[16,32,256]{2,1,0:T(8,128)(2,1)S(1)} %slice.74), channel_id=1, source_target_pairs={{0,6},{1,7},{2,0},{3,1},{4,2},{5,3},{6,4},{7,5},{8,14},{9,15},{10,... | collective-permute-start | bytes 786440 | tf_op jit(solution)/shard_map/ppermute | solution.py:265
  159.9 9.2 %collective-permute-start.13 = (bf16[16,32,256]{2,1,0:T(8,128)(2,1)S(1)}, bf16[16,32,256]{2,1,0:T(8,128)(2,1)S(1)}, u32[]{:S(2)}, u32[]{:S(2)}) collective-permute-start(bf16[16,32,256]{2,1,0:T(8,128)(2,1)S(1)} %slice.74), channel_id=1, source_target_pairs={{0,2},{1,3},{2,4},{3,5},{4,6},{5,7},{6,0},{7,1},{8,10},{9,11},{10,... | collective-permute-start | bytes 786440 | tf_op jit(solution)/shard_map/ppermute | solution.py:265
  170.4 55.5 %collective-permute-start.17 = (bf16[64,32,256]{2,1,0:T(8,128)(2,1)}, bf16[64,32,256]{2,1,0:T(8,128)(2,1)}, u32[]{:S(2)}, u32[]{:S(2)}) collective-permute-start(bf16[64,32,256]{2,1,0:T(8,128)(2,1)} %pad_maximum_fusion.1.refs_9_), channel_id=1, source_target_pairs={{0,384},{8,392},{16,400},{24,408},{32,416},{40,424},{48,432},{56,4... | collective-permute-start | bytes 3145736 | tf_op jit(solution)/shard_map/ppermute | solution.py:262
  175.2 55.2 %collective-permute-start.16 = (bf16[64,32,256]{2,1,0:T(8,128)(2,1)}, bf16[64,32,256]{2,1,0:T(8,128)(2,1)}, u32[]{:S(2)}, u32[]{:S(2)}) collective-permute-start(bf16[64,32,256]{2,1,0:T(8,128)(2,1)} %pad_maximum_fusion.1.refs_9_), channel_id=1, source_target_pairs={{0,128},{8,136},{16,144},{24,152},{32,160},{40,168},{48,176},{56,1... | collective-permute-start | bytes 3145736 | tf_op jit(solution)/shard_map/ppermute | solution.py:262
  177.2 33.4 %collective-permute-start.8 = (bf16[16,40,256]{2,1,0:T(8,128)(2,1)S(1)}, bf16[16,40,256]{2,1,0:T(8,128)(2,1)S(1)}, u32[]{:S(2)}, u32[]{:S(2)}) collective-permute-start(bf16[16,40,256]{2,1,0:T(8,128)(2,1)S(1)} %slice.72), channel_id=1, source_target_pairs={{0,256},{8,264},{16,272},{24,280},{32,288},{40,296},{48,304},{56,3... | collective-permute-start | bytes 983048 | tf_op jit(solution)/shard_map/ppermute | solution.py:262
  181.3 29.3 %collective-permute-start.7 = (bf16[16,40,256]{2,1,0:T(8,128)(2,1)S(1)}, bf16[16,40,256]{2,1,0:T(8,128)(2,1)S(1)}, u32[]{:S(2)}, u32[]{:S(2)}) collective-permute-start(bf16[16,40,256]{2,1,0:T(8,128)(2,1)S(1)} %slice.72), channel_id=1, source_target_pairs={{0,384},{8,392},{16,400},{24,408},{32,416},{40,424},{48,432},{56,4... | collective-permute-start | bytes 983048 | tf_op jit(solution)/shard_map/ppermute | solution.py:262
  184.3 30.8 %collective-permute-start.6 = (bf16[16,40,256]{2,1,0:T(8,128)(2,1)S(1)}, bf16[16,40,256]{2,1,0:T(8,128)(2,1)S(1)}, u32[]{:S(2)}, u32[]{:S(2)}) collective-permute-start(bf16[16,40,256]{2,1,0:T(8,128)(2,1)S(1)} %slice.72), channel_id=1, source_target_pairs={{0,128},{8,136},{16,144},{24,152},{32,160},{40,168},{48,176},{56,1... | collective-permute-start | bytes 983048 | tf_op jit(solution)/shard_map/ppermute | solution.py:262
  215.0 0.7 copy-start.1
  215.8 12.6 %copy-start.13 = (s32[64]{0:T(128)S(1)}, s32[64]{0:T(128)}, u32[]{:S(2)}) copy-start(s32[64]{0:T(128)} %param.15) | copy-start | bytes 772
  216.9 25.2 %collective-permute-start.10 = (bf16[64,32,256]{2,1,0:T(8,128)(2,1)}, bf16[64,32,256]{2,1,0:T(8,128)(2,1)}, u32[]{:S(2)}, u32[]{:S(2)}) collective-permute-start(bf16[64,32,256]{2,1,0:T(8,128)(2,1)} %slice.73.refs_4_), channel_id=1, source_target_pairs={{0,6},{1,7},{2,0},{3,1},{4,2},{5,3},{6,4},{7,5},{8,14},{9,15},{10,... | collective-permute-start | bytes 3145736 | tf_op jit(solution)/shard_map/ppermute | solution.py:265
  220.8 25.2 %collective-permute-start.9 = (bf16[64,32,256]{2,1,0:T(8,128)(2,1)}, bf16[64,32,256]{2,1,0:T(8,128)(2,1)}, u32[]{:S(2)}, u32[]{:S(2)}) collective-permute-start(bf16[64,32,256]{2,1,0:T(8,128)(2,1)} %slice.73.refs_4_), channel_id=1, source_target_pairs={{0,2},{1,3},{2,4},{3,5},{4,6},{5,7},{6,0},{7,1},{8,10},{9,11},{10,... | collective-permute-start | bytes 3145736 | tf_op jit(solution)/shard_map/ppermute | solution.py:265
  224.0 26.1 %collective-permute-start.25 = (bf16[64,32,256]{2,1,0:T(8,128)(2,1)}, bf16[64,32,256]{2,1,0:T(8,128)(2,1)}, u32[]{:S(2)}, u32[]{:S(2)}) collective-permute-start(bf16[64,32,256]{2,1,0:T(8,128)(2,1)} %pad_maximum_fusion.1.refs_9_), channel_id=1, source_target_pairs={{0,1},{1,0},{2,3},{3,2},{4,5},{5,4},{6,7},{7,6},{8,9},{9,8},{10,11... | collective-permute-start | bytes 3145736 | tf_op jit(solution)/shard_map/ppermute | solution.py:292
  225.9 26.6 %collective-permute-start.20 = (bf16[64,32,256]{2,1,0:T(8,128)(2,1)}, bf16[64,32,256]{2,1,0:T(8,128)(2,1)}, u32[]{:S(2)}, u32[]{:S(2)}) collective-permute-start(bf16[64,32,256]{2,1,0:T(8,128)(2,1)} %slice.73.refs_4_), channel_id=1, source_target_pairs={{0,1},{1,0},{2,3},{3,2},{4,5},{5,4},{6,7},{7,6},{8,9},{9,8},{10,11... | collective-permute-start | bytes 3145736 | tf_op jit(solution)/shard_map/ppermute | solution.py:292
  228.5 5.1 %copy-start.2 = (bf16[16,40,256]{2,1,0:T(8,128)(2,1)S(1)}, bf16[16,40,256]{2,1,0:T(8,128)(2,1)}, u32[]{:S(2)}) copy-start(bf16[16,40,256]{2,1,0:T(8,128)(2,1)} %copy-done.1) | copy-start | bytes 983044
  230.4 24.8 %collective-permute-start.19 = (bf16[32,32,256]{2,1,0:T(8,128)(2,1)}, bf16[32,32,256]{2,1,0:T(8,128)(2,1)}, u32[]{:S(2)}, u32[]{:S(2)}) collective-permute-start(bf16[32,32,256]{2,1,0:T(8,128)(2,1)} %slice.76), channel_id=1, source_target_pairs={{0,384},{8,392},{16,400},{24,408},{32,416},{40,424},{48,432},{56,4... | collective-permute-start | bytes 1572872 | tf_op jit(solution)/shard_map/ppermute | solution.py:262
  242.1 17.5 %collective-permute-start.18 = (bf16[32,32,256]{2,1,0:T(8,128)(2,1)S(1)}, bf16[32,32,256]{2,1,0:T(8,128)(2,1)S(1)}, u32[]{:S(2)}, u32[]{:S(2)}) collective-permute-start(bf16[32,32,256]{2,1,0:T(8,128)(2,1)S(1)} %slice.75), channel_id=1, source_target_pairs={{0,128},{8,136},{16,144},{24,152},{32,160},{40,168},{48,176},{56,1... | collective-permute-start | bytes 1572872 | tf_op jit(solution)/shard_map/ppermute | solution.py:262
  246.0 27.8 %collective-permute-start.27 = (bf16[64,32,256]{2,1,0:T(8,128)(2,1)}, bf16[64,32,256]{2,1,0:T(8,128)(2,1)S(1)}, u32[]{:S(2)}, u32[]{:S(2)}) collective-permute-start(bf16[64,32,256]{2,1,0:T(8,128)(2,1)} %collective-permute-done.17.refs_11_), channel_id=1, source_target_pairs={{0,1},{1,0},{2,3},{3,2},{4,5},{5,4},{6,7},{7,6},{8,9},{9,8},{10,11... | collective-permute-start | bytes 3145736 | tf_op jit(solution)/shard_map/ppermute | solution.py:292
  250.1 25.7 %collective-permute-start.26 = (bf16[64,32,256]{2,1,0:T(8,128)(2,1)}, bf16[64,32,256]{2,1,0:T(8,128)(2,1)S(1)}, u32[]{:S(2)}, u32[]{:S(2)}) collective-permute-start(bf16[64,32,256]{2,1,0:T(8,128)(2,1)} %collective-permute-done.16.refs_10_), channel_id=1, source_target_pairs={{0,1},{1,0},{2,3},{3,2},{4,5},{5,4},{6,7},{7,6},{8,9},{9,8},{10,11... | collective-permute-start | bytes 3145736 | tf_op jit(solution)/shard_map/ppermute | solution.py:292
  252.5 16.9 %collective-permute-start.12 = (bf16[32,32,256]{2,1,0:T(8,128)(2,1)S(1)}, bf16[32,32,256]{2,1,0:T(8,128)(2,1)S(1)}, u32[]{:S(2)}, u32[]{:S(2)}) collective-permute-start(bf16[32,32,256]{2,1,0:T(8,128)(2,1)S(1)} %slice.60), channel_id=1, source_target_pairs={{0,6},{1,7},{2,0},{3,1},{4,2},{5,3},{6,4},{7,5},{8,14},{9,15},{10,... | collective-permute-start | bytes 1572872 | tf_op jit(solution)/shard_map/ppermute | solution.py:265
  255.3 16.1 %collective-permute-start.11 = (bf16[32,32,256]{2,1,0:T(8,128)(2,1)S(1)}, bf16[32,32,256]{2,1,0:T(8,128)(2,1)S(1)}, u32[]{:S(2)}, u32[]{:S(2)}) collective-permute-start(bf16[32,32,256]{2,1,0:T(8,128)(2,1)S(1)} %slice.59), channel_id=1, source_target_pairs={{0,2},{1,3},{2,4},{3,5},{4,6},{5,7},{6,0},{7,1},{8,10},{9,11},{10,... | collective-permute-start | bytes 1572872 | tf_op jit(solution)/shard_map/ppermute | solution.py:265
  259.6 22.4 %copy-start.6 = (bf16[32,32,256]{2,1,0:T(8,128)(2,1)}, bf16[32,32,256]{2,1,0:T(8,128)(2,1)S(1)}, u32[]{:S(2)}) copy-start(bf16[32,32,256]{2,1,0:T(8,128)(2,1)S(1)} %collective-permute-done.18.refs_12_) | copy-start | bytes 1572868
  259.6 18.6 %collective-permute-start.29 = (bf16[32,32,256]{2,1,0:T(8,128)(2,1)}, bf16[32,32,256]{2,1,0:T(8,128)(2,1)S(1)}, u32[]{:S(2)}, u32[]{:S(2)}) collective-permute-start(bf16[32,32,256]{2,1,0:T(8,128)(2,1)} %collective-permute-done.19.refs_13_), channel_id=1, source_target_pairs={{0,1},{1,0},{2,3},{3,2},{4,5},{5,4},{6,7},{7,6},{8,9},{9,8},{10,11... | collective-permute-start | bytes 1572872 | tf_op jit(solution)/shard_map/ppermute | solution.py:292
  269.5 12.6 %copy-start.7 = (bf16[32,32,256]{2,1,0:T(8,128)(2,1)}, bf16[32,32,256]{2,1,0:T(8,128)(2,1)S(1)}, u32[]{:S(2)}) copy-start(bf16[32,32,256]{2,1,0:T(8,128)(2,1)S(1)} %collective-permute-done.12.refs_8_) | copy-start | bytes 1572868
  269.5 12.6 %collective-permute-start.21 = (bf16[64,32,256]{2,1,0:T(8,128)(2,1)}, bf16[64,32,256]{2,1,0:T(8,128)(2,1)S(1)}, u32[]{:S(2)}, u32[]{:S(2)}) collective-permute-start(bf16[64,32,256]{2,1,0:T(8,128)(2,1)} %collective-permute-done.9.refs_5_), channel_id=1, source_target_pairs={{0,1},{1,0},{2,3},{3,2},{4,5},{5,4},{6,7},{7,6},{8,9},{9,8},{10,11... | collective-permute-start | bytes 3145736 | tf_op jit(solution)/shard_map/ppermute | solution.py:292
  271.4 10.7 %copy-start.8 = (bf16[32,32,256]{2,1,0:T(8,128)(2,1)}, bf16[32,32,256]{2,1,0:T(8,128)(2,1)S(1)}, u32[]{:S(2)}) copy-start(bf16[32,32,256]{2,1,0:T(8,128)(2,1)S(1)} %collective-permute-done.11.refs_7_) | copy-start | bytes 1572868
  271.4 12.4 %collective-permute-start.22 = (bf16[64,32,256]{2,1,0:T(8,128)(2,1)}, bf16[64,32,256]{2,1,0:T(8,128)(2,1)}, u32[]{:S(2)}, u32[]{:S(2)}) collective-permute-start(bf16[64,32,256]{2,1,0:T(8,128)(2,1)} %collective-permute-done.10.refs_6_), channel_id=1, source_target_pairs={{0,1},{1,0},{2,3},{3,2},{4,5},{5,4},{6,7},{7,6},{8,9},{9,8},{10,11... | collective-permute-start | bytes 3145736 | tf_op jit(solution)/shard_map/ppermute | solution.py:292
  273.8 10.0 %copy-start.3 = (bf16[64,32,256]{2,1,0:T(8,128)(2,1)}, bf16[64,32,256]{2,1,0:T(8,128)(2,1)S(1)}, u32[]{:S(2)}) copy-start(bf16[64,32,256]{2,1,0:T(8,128)(2,1)S(1)} %collective-permute-done.27.refs_21_) | copy-start | bytes 3145732
  273.9 6.5 %collective-permute-start.28 = (bf16[32,32,256]{2,1,0:T(8,128)(2,1)S(1)}, bf16[32,32,256]{2,1,0:T(8,128)(2,1)S(1)}, u32[]{:S(2)}, u32[]{:S(2)}) collective-permute-start(bf16[32,32,256]{2,1,0:T(8,128)(2,1)S(1)} %collective-permute-done.18.refs_12_), channel_id=1, source_target_pairs={{0,1},{1,0},{2,3},{3,2},{4,5},{5,4},{6,7},{7,6},{8,9},{9,8},{10,11... | collective-permute-start | bytes 1572872 | tf_op jit(solution)/shard_map/ppermute | solution.py:292
  275.8 6.3 %copy-start.4 = (bf16[64,32,256]{2,1,0:T(8,128)(2,1)}, bf16[64,32,256]{2,1,0:T(8,128)(2,1)S(1)}, u32[]{:S(2)}) copy-start(bf16[64,32,256]{2,1,0:T(8,128)(2,1)S(1)} %collective-permute-done.26.refs_20_) | copy-start | bytes 3145732
  275.8 4.6 %collective-permute-start.24 = (bf16[32,32,256]{2,1,0:T(8,128)(2,1)S(1)}, bf16[32,32,256]{2,1,0:T(8,128)(2,1)S(1)}, u32[]{:S(2)}, u32[]{:S(2)}) collective-permute-start(bf16[32,32,256]{2,1,0:T(8,128)(2,1)S(1)} %collective-permute-done.12.refs_8_), channel_id=1, source_target_pairs={{0,1},{1,0},{2,3},{3,2},{4,5},{5,4},{6,7},{7,6},{8,9},{9,8},{10,11... | collective-permute-start | bytes 1572872 | tf_op jit(solution)/shard_map/ppermute | solution.py:292
  278.2 3.9 copy-start.9
  278.2 3.8 collective-permute-start.23
  280.4 1.7 copy-start.10
  280.4 1.7 copy-start.11
  282.0 0.8 copy-start.12
  282.8 1.0 copy-start.5
  283.8 1.4 copy-start
